TPU v7x, 32 devices: a whole 2x2x4 slice. The times are simulated.
32 devices in a mesh: rep: 4 (over y, x), shard: 8 (over z, core).
Axes of the slice: x: 2, y: 2, z: 4, core: 2. Of those that a mesh axis runs over, the one named last changes fastest.
Arguments:
- tokens: bfloat16 [32, 512, 1024], P(('rep', 'shard')), may hold values from -6 to 6
- cotangent: bfloat16 [32, 512, 1024], P(('rep', 'shard')), may hold values from -6 to 6
- lengths: int32 [32], replicated, may hold values from 1 to 512, 12288 in all
- slot_sequence: int32 [32], P(('rep', 'shard')), may hold values from 0 to 31, each once
- step_count: int32 [1], replicated, may hold values from 1 to 20
- learn_rate: float32 [1], replicated, may hold values from 0.1 to 1
- attention_in: float32 [1024, 3, 1024], P('shard'), may hold values from -0.1875 to 0.1875
- attention_in_first: float32 [1024, 3, 1024], P('shard'), may hold values from -36 to 36
- attention_in_second: float32 [1024, 3, 1024], P('shard'), may hold values from 20 to 400
- attention_out: float32 [1024, 1024], P('shard'), may hold values from -1.5 to 1.5
- attention_out_first: float32 [1024, 1024], P('shard'), may hold values from -36 to 36
- attention_out_second: float32 [1024, 1024], P('shard'), may hold values from 20 to 400
- gate_up_weight: float32 [1024, 2, 2816], P('shard'), may hold values from -0.1875 to 0.1875
- gate_up_first: float32 [1024, 2, 2816], P('shard'), may hold values from -36 to 36
- gate_up_second: float32 [1024, 2, 2816], P('shard'), may hold values from 20 to 400
- down_weight: float32 [2816, 1024], P('shard'), may hold values from -0.109375 to 0.109375
- down_first: float32 [2816, 1024], P('shard'), may hold values from -36 to 36
- down_second: float32 [2816, 1024], P('shard'), may hold values from 20 to 400
Outputs:
- output: bfloat16 [32, 512, 1024], P(('rep', 'shard'))
- input_grad: float32 [32, 512, 1024], P(('rep', 'shard'))
- attention_in_grad: float32 [1024, 3, 1024], P('shard')
- attention_in_new: float32 [1024, 3, 1024], P('shard')
- attention_in_first_new: float32 [1024, 3, 1024], P('shard')
- attention_in_second_new: float32 [1024, 3, 1024], P('shard')
- attention_out_grad: float32 [1024, 1024], P('shard')
- attention_out_new: float32 [1024, 1024], P('shard')
- attention_out_first_new: float32 [1024, 1024], P('shard')
- attention_out_second_new: float32 [1024, 1024], P('shard')
- gate_up_grad: float32 [1024, 2, 2816], P('shard')
- gate_up_new: float32 [1024, 2, 2816], P('shard')
- gate_up_first_new: float32 [1024, 2, 2816], P('shard')
- gate_up_second_new: float32 [1024, 2, 2816], P('shard')
- down_grad: float32 [2816, 1024], P('shard')
- down_new: float32 [2816, 1024], P('shard')
- down_first_new: float32 [2816, 1024], P('shard')
- down_second_new: float32 [2816, 1024], P('shard')
Inputs may be any that keep to these rules, and one draw needn't show every extreme that they name: `lengths`: lengths of the sequences by number; they add up to 3 / 4 of 16384, and one is exactly 512. `slot_sequence`: A permutation of the 32 sequence numbers.
All inputs are finite; a program needn't handle non-finite values.
Results may differ from a plain program's by a relative error of at most 0.025.
The roundings to bfloat16 on the way count: a program that leaves them out, or rounds other values in their place, can miss the bound.
Values may be sent and summed in bfloat16 or wider, within the bound.
A program may use at most 256 MiB of HBM per device.

v0:
```python
import jax
import jax.numpy as jnp
from jax import lax
from jax.sharding import PartitionSpec as P

HD = 64


norm_eps = 1e-05
beta_first = 0.9
beta_second = 0.95
adam_eps = 1e-08
weight_decay = 0.1
rope_base = 10000.0
masked_score = -1e30


def layer_norm(values):
    centered = values - jnp.mean(values, axis=-1, keepdims=True)
    inverse = lax.rsqrt(jnp.mean(centered * centered, axis=-1, keepdims=True) + norm_eps)
    return (centered * inverse, inverse)


def norm_back(normed, inverse, upstream):
    mean_grad = jnp.mean(upstream, axis=-1, keepdims=True)
    mean_dot = jnp.mean(upstream * normed, axis=-1, keepdims=True)
    return inverse * (upstream - mean_grad - normed * mean_dot)


def rope_tables(position_count, head_size):
    half_size = head_size // 2
    frequency = rope_base ** (-(jnp.arange(half_size, dtype=jnp.float32) * 2.0 / head_size))
    angles = jnp.arange(position_count, dtype=jnp.float32)[:, None] * frequency[None, :]
    angles = jnp.concatenate([angles, angles], axis=1)
    return (jnp.cos(angles)[:, None, :], jnp.sin(angles)[:, None, :])


def rotate(values, cosine_table, sine_table):
    half_size = values.shape[-1] // 2
    turned = jnp.concatenate([-values[..., half_size:], values[..., :half_size]], axis=-1)
    return values * cosine_table + turned * sine_table


def masked_scores(queries, rotated_keys, length):
    position_count, head_size = (queries.shape[0], queries.shape[-1])
    scores = jnp.einsum(
        "qhd,khd->hqk", queries, rotated_keys, preferred_element_type=jnp.float32
    ) * head_size ** (-0.5)
    position = jnp.arange(position_count)
    allowed = (position[None, :] <= position[:, None]) & (position[None, :] < length)
    return jnp.where(allowed[None], scores, masked_score)


def attend_forward(pieces):
    queries, rotated_keys, values_low, length = pieces
    scores = masked_scores(queries, rotated_keys, length)
    row_max = jnp.max(scores, axis=-1, keepdims=True)
    exponent = jnp.exp(scores - row_max)
    row_sum = jnp.sum(exponent, axis=-1, keepdims=True)
    weights = (exponent / row_sum).astype(jnp.bfloat16)
    mixed_heads = jnp.einsum(
        "hqk,khd->qhd", weights, values_low, preferred_element_type=jnp.float32
    )
    return (mixed_heads, row_max + jnp.log(row_sum))


def attend_backward(pieces):
    queries, rotated_keys, values_low, length, log_total, mixed_grad = pieces
    head_size = queries.shape[-1]
    scores = masked_scores(queries, rotated_keys, length)
    probability = jnp.exp(scores - log_total)
    value_grad = jnp.einsum(
        "hqk,qhd->khd",
        probability.astype(jnp.bfloat16),
        mixed_grad,
        preferred_element_type=jnp.float32,
    )
    probability_grad = jnp.einsum(
        "qhd,khd->hqk", mixed_grad, values_low, preferred_element_type=jnp.float32
    )
    inner_dot = jnp.sum(probability * probability_grad, axis=-1, keepdims=True)
    score_grad = (probability * (probability_grad - inner_dot) * head_size ** (-0.5)).astype(
        jnp.bfloat16
    )
    query_grad = jnp.einsum(
        "hqk,khd->qhd", score_grad, rotated_keys, preferred_element_type=jnp.float32
    )
    key_grad = jnp.einsum("hqk,qhd->khd", score_grad, queries, preferred_element_type=jnp.float32)
    return (query_grad, key_grad, value_grad)


def adam_update(weight, first, second, gradient, step_count, learn_rate):
    steps_taken = step_count[0].astype(jnp.float32)
    first_new = beta_first * first + (1.0 - beta_first) * gradient
    second_new = beta_second * second + (1.0 - beta_second) * gradient * gradient
    first_hat = first_new / (1.0 - beta_first**steps_taken)
    second_hat = second_new / (1.0 - beta_second**steps_taken)
    weight_new = weight - learn_rate[0] * (
        first_hat / (jnp.sqrt(second_hat) + adam_eps) + weight_decay * weight
    )
    return (gradient, weight_new, first_new, second_new)


def shards(
    tokens,
    cotangent,
    lengths,
    slot_sequence,
    step_count,
    learn_rate,
    attention_in,
    attention_in_first,
    attention_in_second,
    attention_out,
    attention_out_first,
    attention_out_second,
    gate_up_weight,
    gate_up_first,
    gate_up_second,
    down_weight,
    down_first,
    down_second,
):
    slot_count, position_count, feature_count = tokens.shape
    row_total = slot_count * position_count
    head_count = feature_count // HD
    shaped = (slot_count, position_count, head_count, HD)
    inputs = tokens.astype(jnp.float32).reshape(row_total, feature_count)
    matches = jnp.arange(lengths.shape[0])[None, :] == slot_sequence[:, None]
    slot_length = jnp.sum(jnp.where(matches, lengths[None, :], 0), axis=1)
    alive_rows = (
        (jnp.arange(position_count)[None, :] < slot_length[:, None])
        .astype(jnp.float32)
        .reshape(row_total, 1)
    )
    cosine_table, sine_table = rope_tables(position_count, HD)
    in_local = attention_in.astype(jnp.bfloat16)
    out_local = attention_out.astype(jnp.bfloat16)
    gate_up_local = gate_up_weight.astype(jnp.bfloat16)
    down_local = down_weight.astype(jnp.bfloat16)
    in_full, out_full = (
        lax.all_gather(in_local, "shard", axis=0, tiled=True),
        lax.all_gather(out_local, "shard", axis=0, tiled=True),
    )
    normed_one, inverse_one = layer_norm(inputs)
    first_input = normed_one.astype(jnp.bfloat16)
    projected = jnp.einsum("rd,dke->rke", first_input, in_full, preferred_element_type=jnp.float32)
    queries = rotate(projected[:, 0].reshape(shaped), cosine_table, sine_table).astype(jnp.bfloat16)
    rotated_keys = rotate(projected[:, 1].reshape(shaped), cosine_table, sine_table).astype(
        jnp.bfloat16
    )
    values_low = projected[:, 2].reshape(shaped).astype(jnp.bfloat16)
    mixed_heads, log_total = lax.map(
        attend_forward, (queries, rotated_keys, values_low, slot_length)
    )
    mixed_low = mixed_heads.reshape(row_total, feature_count).astype(jnp.bfloat16)
    residual = inputs + jnp.dot(mixed_low, out_full, preferred_element_type=jnp.float32)
    normed_two, inverse_two = layer_norm(residual)
    second_input = normed_two.astype(jnp.bfloat16)
    gate_up_full, down_full = (
        lax.all_gather(gate_up_local, "shard", axis=0, tiled=True),
        lax.all_gather(down_local, "shard", axis=0, tiled=True),
    )
    gate_up = jnp.einsum(
        "rd,dkf->rkf", second_input, gate_up_full, preferred_element_type=jnp.float32
    )
    gate_value = gate_up[:, 0]
    up_value = gate_up[:, 1]
    sigmoid_gate = jax.nn.sigmoid(gate_value)
    hidden_low = (gate_value * sigmoid_gate * up_value).astype(jnp.bfloat16)
    result = residual + jnp.dot(hidden_low, down_full, preferred_element_type=jnp.float32)
    output = (result * alive_rows).astype(jnp.bfloat16).reshape(tokens.shape)
    output_grad = cotangent.astype(jnp.float32).reshape(row_total, feature_count) * alive_rows
    result_grad_low = output_grad.astype(jnp.bfloat16)
    gate_up_full, down_full = (
        lax.all_gather(gate_up_local, "shard", axis=0, tiled=True),
        lax.all_gather(down_local, "shard", axis=0, tiled=True),
    )
    hidden_grad = jnp.einsum(
        "rd,fd->rf", result_grad_low, down_full, preferred_element_type=jnp.float32
    )
    gate_grad = hidden_grad * up_value * sigmoid_gate * (1.0 + gate_value * (1.0 - sigmoid_gate))
    up_grad = hidden_grad * gate_value * sigmoid_gate
    gate_up_grad_low = jnp.stack([gate_grad, up_grad], axis=1).astype(jnp.bfloat16)
    second_input_grad = jnp.einsum(
        "rkf,dkf->rd", gate_up_grad_low, gate_up_full, preferred_element_type=jnp.float32
    )
    residual_grad = output_grad + norm_back(normed_two, inverse_two, second_input_grad)
    columns = hidden_low
    down_part = lax.psum_scatter(
        jnp.einsum("rc,rd->cd", columns, result_grad_low, preferred_element_type=jnp.float32),
        "shard",
        scatter_dimension=0,
        tiled=True,
    )
    columns = second_input
    gate_up_part = lax.psum_scatter(
        jnp.einsum("rc,rkf->ckf", columns, gate_up_grad_low, preferred_element_type=jnp.float32),
        "shard",
        scatter_dimension=0,
        tiled=True,
    )
    branch_grad = residual_grad.astype(jnp.bfloat16)
    in_full, out_full = (
        lax.all_gather(in_local, "shard", axis=0, tiled=True),
        lax.all_gather(out_local, "shard", axis=0, tiled=True),
    )
    mixed_grad = (
        jnp.einsum("re,de->rd", branch_grad, out_full, preferred_element_type=jnp.float32)
        .astype(jnp.bfloat16)
        .reshape(shaped)
    )
    query_grad, key_grad, value_grad = lax.map(
        attend_backward, (queries, rotated_keys, values_low, slot_length, log_total, mixed_grad)
    )
    query_back = rotate(query_grad, cosine_table, -sine_table).reshape(row_total, feature_count)
    key_back = rotate(key_grad, cosine_table, -sine_table).reshape(row_total, feature_count)
    projected_grad = jnp.stack(
        [query_back, key_back, value_grad.reshape(row_total, feature_count)], axis=1
    ).astype(jnp.bfloat16)
    first_input_grad = jnp.einsum(
        "rke,dke->rd", projected_grad, in_full, preferred_element_type=jnp.float32
    )
    input_grad = (residual_grad + norm_back(normed_one, inverse_one, first_input_grad)).reshape(
        tokens.shape
    )
    inner_part = jnp.einsum(
        "rc,rke->cke", first_input, projected_grad, preferred_element_type=jnp.float32
    )
    outer_part = jnp.einsum("rc,re->ce", mixed_low, branch_grad, preferred_element_type=jnp.float32)
    attention_part = lax.psum_scatter(
        jnp.concatenate([inner_part, outer_part[:, None]], axis=1),
        "shard",
        scatter_dimension=0,
        tiled=True,
    )
    attention_part, gate_up_part, down_part = lax.psum(
        (attention_part, gate_up_part, down_part), "rep"
    )
    in_grad, in_new, in_first, in_second = adam_update(
        attention_in,
        attention_in_first,
        attention_in_second,
        attention_part[:, :3],
        step_count,
        learn_rate,
    )
    out_grad, out_new, out_first, out_second = adam_update(
        attention_out,
        attention_out_first,
        attention_out_second,
        attention_part[:, 3],
        step_count,
        learn_rate,
    )
    gu_grad, gu_new, gu_first, gu_second = adam_update(
        gate_up_weight, gate_up_first, gate_up_second, gate_up_part, step_count, learn_rate
    )
    dn_grad, dn_new, dn_first, dn_second = adam_update(
        down_weight, down_first, down_second, down_part, step_count, learn_rate
    )
    return (
        output,
        input_grad,
        in_grad,
        in_new,
        in_first,
        in_second,
        out_grad,
        out_new,
        out_first,
        out_second,
        gu_grad,
        gu_new,
        gu_first,
        gu_second,
        dn_grad,
        dn_new,
        dn_first,
        dn_second,
    )


def solution(mesh):
    return jax.shard_map(
        shards,
        mesh=mesh,
        in_specs=(
            P(("rep", "shard"), None, None),
            P(("rep", "shard"), None, None),
            P(),
            P(("rep", "shard")),
            P(),
            P(),
            P("shard", None, None),
            P("shard", None, None),
            P("shard", None, None),
            P("shard", None),
            P("shard", None),
            P("shard", None),
            P("shard", None, None),
            P("shard", None, None),
            P("shard", None, None),
            P("shard", None),
            P("shard", None),
            P("shard", None),
        ),
        out_specs=(
            P(("rep", "shard"), None, None),
            P(("rep", "shard"), None, None),
            P("shard", None, None),
            P("shard", None, None),
            P("shard", None, None),
            P("shard", None, None),
            P("shard", None),
            P("shard", None),
            P("shard", None),
            P("shard", None),
            P("shard", None, None),
            P("shard", None, None),
            P("shard", None, None),
            P("shard", None, None),
            P("shard", None),
            P("shard", None),
            P("shard", None),
            P("shard", None),
        ),
        check_vma=False,
    )
```

profile of v0, /device:TPU:0, one launch (start us, length us, event | category | flops | bytes accessed | tf_op | source)
XLA Modules:
  0.0 988.6 jit_solution(14315192058969197153)
XLA Ops:
  19.0 58.7 %all-gather.5.cloned.1.call-done = bf16[1024,3,1024]{2,0,1:T(8,128)(2,1)} async-done(((bf16[128,3,1024]{2,0,1:T(8,128)(2,1)}), bf16[1024,3,1024]{2,0,1:T(8,128)(2,1)}) %all-gather.5.cloned.1.call-update) | async-done | bytes 6291472 | tf_op jit(solution)/shard_map/all_gather | solution.py:142
  77.7 5.7 fusion.114
  97.5 7.5 fusion.122
  105.0 8.4 fusion.4
  113.5 10.1 %fusion.69 = bf16[16,64,512]{2,1,0:T(8,128)(2,1)} fusion(bf16[512,16,64]{0,2,1:T(8,128)(2,1)S(1)} %bitcast.224, f32[16,512,512]{1,2,0:T(8,128)} %get-tuple-element.146, f32[16,512]{1,0:T(8,128)S(1)} %fusion.4, f32[16,512]{1,0:T(8,128)S(1)} %get-tuple-element.145), kind=kOutput, calls=%fused_computation.104 | convolution fusion | flops 549978112 | bytes 18939904 | tf_op jit(solution)/shard_map/while/body/eval_jaxpr/hqk,khd->qhd/dot_general | solution.py:61
  127.2 90.3 %all-gather.9.cloned.1.call-done = bf16[1024,2,2816]{2,0,1:T(8,128)(2,1)} async-done(((bf16[128,2,2816]{2,0,1:T(8,128)(2,1)}), bf16[1024,2,2816]{2,0,1:T(8,128)(2,1)}) %all-gather.9.cloned.1.call-update) | async-done | bytes 11534352 | tf_op jit(solution)/shard_map/all_gather | solution.py:161
  217.5 9.4 fusion.98
  231.2 6.3 fusion.30
  238.2 40.1 %all-gather.11.cloned.1.call-done = bf16[2816,1024]{1,0:T(8,128)(2,1)} async-done(((bf16[352,1024]{1,0:T(8,128)(2,1)}), bf16[2816,1024]{1,0:T(8,128)(2,1)}) %all-gather.11.cloned.1.call-update) | async-done | bytes 5767184 | tf_op jit(solution)/shard_map/all_gather | solution.py:162
  278.3 11.2 %fusion.36 = (bf16[512,1,2816]{2,0,1:T(8,128)(2,1)}, bf16[512,1,2816]{2,0,1:T(8,128)(2,1)}) fusion(f32[512,2,2816]{2,0,1:T(8,128)} %copy-done, bf16[2816,1024]{1,0:T(8,128)(2,1)} %all-gather.11.cloned.1.call-done, bf16[1,512,1024]{2,1,0:T(8,128)(2,1)} %param.19, f32[512]{0:T(512)S(1)} %fusion.112), kind=kOutput, calls=%fused_computation.48 | convolution fusion | flops 2973106176 | bytes 24119296 | tf_op jit(solution)/shard_map/rd,fd->rf/dot_general | solution.py:179
  289.5 11.9 %bitcast_reduce_fusion.1 = (f32[512]{0:T(512)S(1)}, f32[512]{0:T(512)S(1)}, f32[512,1024,1]{1,0,2:T(8,128)S(1)}) fusion(f32[512]{0:T(512)S(1)} %add_rsqrt_fusion, f32[512,1024]{1,0:T(8,128)S(1)} %get-tuple-element.148, f32[512]{0:T(512)S(1)} %broadcast_multiply_fusion.4, bf16[1024,2,2816]{2,0,1:T(8,128)(2,1)} %all-gather.9.cloned.1.call-done, ...), kind=kOutput, calls=%fused_computation.93 | convolution fusion | flops 5911084032 | bytes 21504000 | tf_op jit(solution)/shard_map/rkf,dkf->rd/dot_general | solution.py:185
  309.4 9.9 %fusion.70 = bf16[16,64,512]{2,1,0:T(8,128)(2,1)} fusion(bf16[512,16,64]{0,2,1:T(8,128)(2,1)} %bitcast.219, f32[16,512,512]{1,2,0:T(8,128)} %get-tuple-element.146, f32[16,512]{1,0:T(8,128)S(1)} %log_add_fusion), kind=kOutput, calls=%fused_computation.106 | convolution fusion | flops 545783808 | bytes 18907136 | tf_op jit(solution)/shard_map/while/body/eval_jaxpr/hqk,qhd->khd/dot_general | solution.py:72
  321.6 9.7 fusion.126
  331.2 25.0 %fusion.15 = f32[16,64,512]{2,1,0:T(8,128)} fusion(bf16[512,16,64]{0,2,1:T(8,128)(2,1)} %copy-done.18, f32[16,512,512]{1,2,0:T(8,128)} %fusion.126, f32[16,512,512]{1,2,0:T(8,128)} %get-tuple-element.146, f32[16,512]{1,0:T(8,128)S(1)} %log_add_fusion), kind=kOutput, calls=%fused_computation.16 | convolution fusion | flops 566239744 | bytes 36732928 | tf_op jit(solution)/shard_map/while/body/eval_jaxpr/hqk,khd->qhd/dot_general | solution.py:85
  359.4 24.9 %fusion.12 = f32[16,64,512]{2,1,0:T(8,128)} fusion(bf16[512,16,64]{0,2,1:T(8,128)(2,1)} %copy-done.17, f32[16,512,512]{1,2,0:T(8,128)} %fusion.126, f32[16,512,512]{1,2,0:T(8,128)} %get-tuple-element.146, f32[16,512]{1,0:T(8,128)S(1)} %log_add_fusion), kind=kOutput, calls=%fused_computation.15 | convolution fusion | flops 566239744 | bytes 36732928 | tf_op jit(solution)/shard_map/while/body/eval_jaxpr/hqk,qhd->khd/dot_general | solution.py:88
  402.9 6.2 pad_maximum_fusion
  409.3 14.0 %fusion.27 = f32[1024,2,2816]{2,0,1:T(8,128)} fusion(bf16[512,1,2816]{2,0,1:T(8,128)(2,1)} %get-tuple-element.127, bf16[512,1,2816]{2,0,1:T(8,128)(2,1)} %get-tuple-element.126, f32[512,1024]{1,0:T(8,128)S(1)} %get-tuple-element.148, f32[512]{0:T(512)S(1)} %add_rsqrt_fusion, f32[512]{0:T(512)S(1)} %broadcast_multiply_fusion.4), kind=kOutput, calls=%fused_computation.36 | convolution fusion | flops 5918687232 | bytes 30937088 | tf_op jit(solution)/shard_map/rc,rkf->ckf/dot_general | solution.py:198
  423.4 153.2 %reduce-scatter.4.cloned.1.call-done = f32[128,4,1024]{2,0,1:T(8,128)} async-done(((f32[1024,4,1024]{2,0,1:T(8,128)}), f32[128,4,1024]{2,0,1:T(8,128)}) %reduce-scatter.4.cloned.1.call-update) | async-done | bytes 2097168 | tf_op jit(solution)/shard_map/reduce_scatter | solution.py:231
  576.6 228.2 %reduce-scatter.6.cloned.1.call-done = f32[128,2,2816]{2,0,1:T(8,128)} async-done(((f32[1024,2,2816]{2,0,1:T(8,128)}), f32[128,2,2816]{2,0,1:T(8,128)}) %reduce-scatter.6.cloned.1.call-update) | async-done | bytes 2883600 | tf_op jit(solution)/shard_map/reduce_scatter | solution.py:197
  806.6 7.7 bitcast_reduce_fusion
  816.3 6.9 fusion.74
  823.2 125.2 %all-reduce.3.cloned.1.call-done = (f32[128,4,1024]{2,0,1:T(8,128)}, f32[128,2,2816]{2,0,1:T(8,128)}, f32[352,1024]{1,0:T(8,128)}) async-done(((f32[128,4,1024]{2,0,1:T(8,128)}, f32[128,2,2816]{2,0,1:T(8,128)}, f32[352,1024]{1,0:T(8,128)}), (f32[128,4,1024]{2,0,1:T(8,128)}, f32[128,2,2816]{2,0,1:T(8,128)}, f32[352,1024]{1,0:T(8,128)})) %all-reduce.3.cloned.1.call-update) | async-done | bytes 6422544 | tf_op jit(solution)/shard_map/psum | solution.py:237
  948.4 5.8 copy.84
  954.1 4.3 multiply_subtract_fusion
  (151 shorter events, 90.7 us)
Async XLA Ops:
  7.2 70.5 %all-gather.5.cloned.1.call-start = ((), (), s32[]{:S(2)}) async-start(), calls=%async_computation.3 | async-start | bytes 7077888 | tf_op jit(solution)/shard_map/all_gather | solution.py:142
  9.8 113.7 %all-gather.7.cloned.1.call-start = ((), (), s32[]{:S(2)}) async-start(), calls=%async_computation.4 | async-start | bytes 2359296 | tf_op jit(solution)/shard_map/all_gather | solution.py:143
  10.7 206.8 %all-gather.9.cloned.1.call-start = ((), (), s32[]{:S(2)}) async-start(), calls=%async_computation.5 | async-start | bytes 12976128 | tf_op jit(solution)/shard_map/all_gather | solution.py:161
  12.0 266.3 %all-gather.11.cloned.1.call-start = ((), (), s32[]{:S(2)}) async-start(), calls=%async_computation.6 | async-start | bytes 6488064 | tf_op jit(solution)/shard_map/all_gather | solution.py:162
  14.5 408.9 %reduce-scatter.8.cloned.1.call-start = ((), (), s32[]{:S(2)}) async-start(), calls=%async_computation.9 | async-start | bytes 12976128 | tf_op jit(solution)/shard_map/reduce_scatter | solution.py:190
  97.5 7.5 copy-start.17
  97.5 7.5 copy-start.18
  105.0 8.4 copy-start.35
  105.0 8.4 copy-start.16
  126.8 282.4 %copy-start.1 = (f32[512,1024]{1,0:T(8,128)}, f32[512,1024]{1,0:T(8,128)S(1)}, u32[]{:S(2)}) copy-start(f32[512,1024]{1,0:T(8,128)S(1)} %get-tuple-element.148) | copy-start | bytes 6291460
  217.5 13.7 %copy-start.27 = (bf16[1,512,1024]{2,1,0:T(8,128)(2,1)S(1)}, bf16[1,512,1024]{2,1,0:T(8,128)(2,1)}, u32[]{:S(2)}) copy-start(bf16[1,512,1024]{2,1,0:T(8,128)(2,1)} %param.19) | copy-start | bytes 3145732
  237.5 339.2 %reduce-scatter.4.cloned.1.call-start = ((), (), s32[]{:S(2)}) async-start(), calls=%async_computation.7 | async-start | bytes 18874368 | tf_op jit(solution)/shard_map/reduce_scatter | solution.py:231
  359.4 26.8 %copy-start.31 = (f32[512,64]{0,1:T(8,128)S(1)}, f32[512,64]{0,1:T(8,128)}, u32[]{:S(2)}) copy-start(f32[512,64]{0,1:T(8,128)} %get-tuple-element.142) | copy-start | bytes 393220
  409.2 395.6 %reduce-scatter.6.cloned.1.call-start = ((), (), s32[]{:S(2)}) async-start(), calls=%async_computation.8 | async-start | bytes 25952256 | tf_op jit(solution)/shard_map/reduce_scatter | solution.py:197
  423.3 525.0 %all-reduce.3.cloned.1.call-start = ((), (), s32[]{:S(2)}) async-start(), calls=%async_computation.10 | async-start | bytes 12845056 | tf_op jit(solution)/shard_map/psum | solution.py:237
  804.8 11.4 %slice-start = ((s8[11534336]{0:T(1024)(128)(4,1)}), s8[3145728]{0:T(1024)(128)(4,1)S(1)}, s32[]{:S(2)}) async-start(s8[11534336]{0:T(1024)(128)(4,1)} %bitcast.213), calls=%async_computation.11 | async-start | bytes 6291456
  806.5 7.7 copy-start.5
  806.5 7.7 copy-start.10
  806.6 9.7 slice-start.1
  806.6 9.7 slice-start.2
  948.4 5.8 copy-start.7
  948.4 5.8 copy-start.8
  966.0 5.3 copy-start.24
  972.5 4.9 copy-start.26
  (25 other events, 77.0 us)
Sparse Core Ops, SparseCore 0:
  10.2 67.4 all-gather.4
  79.8 27.7 all-gather.6
  109.9 107.5 all-gather.8
  219.5 58.7 all-gather.10
  280.4 118.0 reduce-scatter.7
  409.3 167.2 reduce-scatter.3
  579.0 225.8 reduce-scatter.5
  808.6 139.6 all-reduce.2
where the time goes:
time: 998 us; the launch traced here: 989 us
  waiting for transfers between devices  696 us (70%)
  matrix products  173 us (17%)
  other arithmetic  53.4 us (5%)
  local copies, waits for them, and re-layouts  48.9 us (5%)
  between operations  17.4 us (2%)
    reduce_scatter x1, waiting for transfers between devices, shards(): lax.psum_scatter(jnp.einsum('rc,rkf->ckf', columns, gate_up_grad_low, pre...  228 us
    reduce_scatter x1, waiting for transfers between devices, shards(): lax.psum_scatter(jnp.concatenate([inner_part, outer_part[:, None]], axis=...  153 us
    psum x1, waiting for transfers between devices, shards(): lax.psum((attention_part, gate_up_part, down_part), 'rep')  125 us
    all_gather x1, waiting for transfers between devices, shards(): lax.all_gather(gate_up_local, 'shard', axis=0, tiled=True)  90.3 us
    all_gather x1, waiting for transfers between devices, shards(): lax.all_gather(in_local, 'shard', axis=0, tiled=True)  58.7 us
    all_gather x1, waiting for transfers between devices, shards(): lax.all_gather(down_local, 'shard', axis=0, tiled=True)  40.1 us
    unnamed x88, local copies, waits for them, and re-layouts  29.3 us
    dot_general x1, matrix products, attend_backward(): jnp.einsum('hqk,khd->qhd', score_grad, rotated_keys, preferred_element_ty...  25 us
  transfers between devices with their start and end apart: 8, of which 6 were waited for; matrix products, arithmetic and copies ran while one was open for 23% of the time, Pallas kernels for 0%

commit v1 on v0

--- a/solution.py
+++ b/solution.py
@@ -99,6 +99,23 @@
         first_hat / (jnp.sqrt(second_hat) + adam_eps) + weight_decay * weight
     )
     return (gradient, weight_new, first_new, second_new)
+
+
+def gather_full(local, rep_count, rep_index):
+    rows = local.shape[0]
+    flat = local.reshape(rows, -1)
+    width = flat.shape[1] // rep_count
+    piece = lax.dynamic_slice_in_dim(flat, rep_index * width, width, axis=1)
+    column = lax.all_gather(piece, "shard", axis=0, tiled=True)
+    return lax.all_gather(column, "rep", axis=0, tiled=False)
+
+
+def reduce_full(partial):
+    part = lax.psum_scatter(partial, "rep", scatter_dimension=0, tiled=False)
+    part = lax.psum_scatter(part, "shard", scatter_dimension=0, tiled=True)
+    pieces = lax.all_gather(part, "rep", axis=0, tiled=False)
+    rows = pieces.shape[1]
+    return jnp.transpose(pieces, (1, 0, 2)).reshape(rows, -1).astype(jnp.float32)
 
 
 def shards(
@@ -138,13 +155,17 @@
     out_local = attention_out.astype(jnp.bfloat16)
     gate_up_local = gate_up_weight.astype(jnp.bfloat16)
     down_local = down_weight.astype(jnp.bfloat16)
-    in_full, out_full = (
-        lax.all_gather(in_local, "shard", axis=0, tiled=True),
-        lax.all_gather(out_local, "shard", axis=0, tiled=True),
-    )
+    rep_count = lax.axis_size("rep")
+    rep_index = lax.axis_index("rep")
+    in_full = gather_full(in_local, rep_count, rep_index)
+    out_full = gather_full(out_local, rep_count, rep_index)
+    gate_up_full = gather_full(gate_up_local, rep_count, rep_index)
+    down_full = gather_full(down_local, rep_count, rep_index)
     normed_one, inverse_one = layer_norm(inputs)
     first_input = normed_one.astype(jnp.bfloat16)
-    projected = jnp.einsum("rd,dke->rke", first_input, in_full, preferred_element_type=jnp.float32)
+    projected = jnp.einsum(
+        "rd,qde->rqe", first_input, in_full, preferred_element_type=jnp.float32
+    ).reshape(row_total, 3, feature_count)
     queries = rotate(projected[:, 0].reshape(shaped), cosine_table, sine_table).astype(jnp.bfloat16)
     rotated_keys = rotate(projected[:, 1].reshape(shaped), cosine_table, sine_table).astype(
         jnp.bfloat16
@@ -154,59 +175,62 @@
         attend_forward, (queries, rotated_keys, values_low, slot_length)
     )
     mixed_low = mixed_heads.reshape(row_total, feature_count).astype(jnp.bfloat16)
-    residual = inputs + jnp.dot(mixed_low, out_full, preferred_element_type=jnp.float32)
+    residual = inputs + jnp.einsum(
+        "rd,qde->rqe", mixed_low, out_full, preferred_element_type=jnp.float32
+    ).reshape(row_total, feature_count)
     normed_two, inverse_two = layer_norm(residual)
     second_input = normed_two.astype(jnp.bfloat16)
-    gate_up_full, down_full = (
-        lax.all_gather(gate_up_local, "shard", axis=0, tiled=True),
-        lax.all_gather(down_local, "shard", axis=0, tiled=True),
-    )
     gate_up = jnp.einsum(
-        "rd,dkf->rkf", second_input, gate_up_full, preferred_element_type=jnp.float32
-    )
+        "rd,qdf->rqf", second_input, gate_up_full, preferred_element_type=jnp.float32
+    ).reshape(row_total, 2, -1)
     gate_value = gate_up[:, 0]
     up_value = gate_up[:, 1]
     sigmoid_gate = jax.nn.sigmoid(gate_value)
     hidden_low = (gate_value * sigmoid_gate * up_value).astype(jnp.bfloat16)
-    result = residual + jnp.dot(hidden_low, down_full, preferred_element_type=jnp.float32)
+    result = residual + jnp.einsum(
+        "rf,qfe->rqe", hidden_low, down_full, preferred_element_type=jnp.float32
+    ).reshape(row_total, feature_count)
     output = (result * alive_rows).astype(jnp.bfloat16).reshape(tokens.shape)
     output_grad = cotangent.astype(jnp.float32).reshape(row_total, feature_count) * alive_rows
     result_grad_low = output_grad.astype(jnp.bfloat16)
-    gate_up_full, down_full = (
-        lax.all_gather(gate_up_local, "shard", axis=0, tiled=True),
-        lax.all_gather(down_local, "shard", axis=0, tiled=True),
-    )
     hidden_grad = jnp.einsum(
-        "rd,fd->rf", result_grad_low, down_full, preferred_element_type=jnp.float32
+        "rqe,qfe->rf",
+        result_grad_low.reshape(row_total, rep_count, -1),
+        down_full,
+        preferred_element_type=jnp.float32,
     )
     gate_grad = hidden_grad * up_value * sigmoid_gate * (1.0 + gate_value * (1.0 - sigmoid_gate))
     up_grad = hidden_grad * gate_value * sigmoid_gate
-    gate_up_grad_low = jnp.stack([gate_grad, up_grad], axis=1).astype(jnp.bfloat16)
+    gate_up_grad_low = (
+        jnp.concatenate([gate_grad, up_grad], axis=1)
+        .astype(jnp.bfloat16)
+        .reshape(row_total, rep_count, -1)
+    )
     second_input_grad = jnp.einsum(
-        "rkf,dkf->rd", gate_up_grad_low, gate_up_full, preferred_element_type=jnp.float32
+        "rqf,qdf->rd", gate_up_grad_low, gate_up_full, preferred_element_type=jnp.float32
     )
     residual_grad = output_grad + norm_back(normed_two, inverse_two, second_input_grad)
-    columns = hidden_low
-    down_part = lax.psum_scatter(
-        jnp.einsum("rc,rd->cd", columns, result_grad_low, preferred_element_type=jnp.float32),
-        "shard",
-        scatter_dimension=0,
-        tiled=True,
-    )
-    columns = second_input
-    gate_up_part = lax.psum_scatter(
-        jnp.einsum("rc,rkf->ckf", columns, gate_up_grad_low, preferred_element_type=jnp.float32),
-        "shard",
-        scatter_dimension=0,
-        tiled=True,
-    )
+    down_part = reduce_full(
+        jnp.einsum(
+            "rc,rqe->qce",
+            hidden_low,
+            result_grad_low.reshape(row_total, rep_count, -1),
+            preferred_element_type=jnp.float32,
+        ).astype(jnp.bfloat16)
+    )
+    gate_up_part = reduce_full(
+        jnp.einsum(
+            "rc,rqf->qcf", second_input, gate_up_grad_low, preferred_element_type=jnp.float32
+        ).astype(jnp.bfloat16)
+    ).reshape(gate_up_weight.shape)
     branch_grad = residual_grad.astype(jnp.bfloat16)
-    in_full, out_full = (
-        lax.all_gather(in_local, "shard", axis=0, tiled=True),
-        lax.all_gather(out_local, "shard", axis=0, tiled=True),
-    )
     mixed_grad = (
-        jnp.einsum("re,de->rd", branch_grad, out_full, preferred_element_type=jnp.float32)
+        jnp.einsum(
+            "rqe,qde->rd",
+            branch_grad.reshape(row_total, rep_count, -1),
+            out_full,
+            preferred_element_type=jnp.float32,
+        )
         .astype(jnp.bfloat16)
         .reshape(shaped)
     )
@@ -215,33 +239,35 @@
     )
     query_back = rotate(query_grad, cosine_table, -sine_table).reshape(row_total, feature_count)
     key_back = rotate(key_grad, cosine_table, -sine_table).reshape(row_total, feature_count)
-    projected_grad = jnp.stack(
-        [query_back, key_back, value_grad.reshape(row_total, feature_count)], axis=1
-    ).astype(jnp.bfloat16)
+    projected_grad = (
+        jnp.concatenate([query_back, key_back, value_grad.reshape(row_total, feature_count)], axis=1)
+        .astype(jnp.bfloat16)
+        .reshape(row_total, rep_count, -1)
+    )
     first_input_grad = jnp.einsum(
-        "rke,dke->rd", projected_grad, in_full, preferred_element_type=jnp.float32
+        "rqe,qde->rd", projected_grad, in_full, preferred_element_type=jnp.float32
     )
     input_grad = (residual_grad + norm_back(normed_one, inverse_one, first_input_grad)).reshape(
         tokens.shape
     )
-    inner_part = jnp.einsum(
-        "rc,rke->cke", first_input, projected_grad, preferred_element_type=jnp.float32
-    )
-    outer_part = jnp.einsum("rc,re->ce", mixed_low, branch_grad, preferred_element_type=jnp.float32)
-    attention_part = lax.psum_scatter(
-        jnp.concatenate([inner_part, outer_part[:, None]], axis=1),
-        "shard",
-        scatter_dimension=0,
-        tiled=True,
-    )
-    attention_part, gate_up_part, down_part = lax.psum(
-        (attention_part, gate_up_part, down_part), "rep"
+    in_part = reduce_full(
+        jnp.einsum(
+            "rc,rqe->qce", first_input, projected_grad, preferred_element_type=jnp.float32
+        ).astype(jnp.bfloat16)
+    ).reshape(attention_in.shape)
+    out_part = reduce_full(
+        jnp.einsum(
+            "rc,rqe->qce",
+            mixed_low,
+            branch_grad.reshape(row_total, rep_count, -1),
+            preferred_element_type=jnp.float32,
+        ).astype(jnp.bfloat16)
     )
     in_grad, in_new, in_first, in_second = adam_update(
         attention_in,
         attention_in_first,
         attention_in_second,
-        attention_part[:, :3],
+        in_part,
         step_count,
         learn_rate,
     )
@@ -249,7 +275,7 @@
         attention_out,
         attention_out_first,
         attention_out_second,
-        attention_part[:, 3],
+        out_part,
         step_count,
         learn_rate,
     )

time: 998 us -> 937 us (0.939)
  waiting for transfers between devices: 696 us -> 493 us
  local copies, waits for them, and re-layouts: 48.9 us -> 134 us
  blocking collectives: 0 us -> 55.3 us
    reduce_scatter x3 -> x2, waiting for transfers between devices: 381 us -> 50.8 us  [reduce_full(): part = lax.psum_scatter(part, 'shard', scatter_dimension=0, tiled=True)]
    unnamed x8 -> x22, waiting for transfers between devices: 0.13 us -> 195 us
    psum x1 -> x0, waiting for transfers between devices: 125 us -> none  [shards(): lax.psum((attention_part, gate_up_part, down_part), 'rep')]
    all_gather x4 -> x8, waiting for transfers between devices: 189 us -> 248 us  [the longest x4 183 us: gather_full(): return lax.all_gather(column, 'rep', axis=0, tiled=False)]
    all_gather x0 -> x4, blocking collectives: none -> 55.3 us  [the longest x3 35.9 us: reduce_full(): pieces = lax.all_gather(part, 'rep', axis=0, tiled=False)]
    unnamed x88 -> x108, local copies, waits for them, and re-layouts: 29.3 us -> 59.1 us
    dot_general x0 -> x3, local copies, waits for them, and re-layouts: none -> 21.3 us  [the longest x1 9.03 us: shards(): jnp.einsum('rd,qde->rqe', first_input, in_full, preferred_element_type=jn...]
    convert_element_type x1 -> x11, local copies, waits for them, and re-layouts: 2.27 us -> 17.4 us  [the longest x7 12.3 us: reduce_full(): jnp.transpose(pieces, (1, 0, 2)).reshape(rows, -1).astype(jnp.float32)]
  transfers between devices with their start and end apart: 8 -> 16, of which waited for: 6 -> 15; matrix products, arithmetic and copies ran while one was open for 23% -> 31% of each run, Pallas kernels for 0% -> 0%
where the time goes in v1:
time: 937 us; the launch traced here: 931 us
  waiting for transfers between devices  493 us (53%)
  matrix products  169 us (18%)
  local copies, waits for them, and re-layouts  134 us (14%)
  other arithmetic  61.3 us (7%)
  blocking collectives  55.3 us (6%)
  between operations  17 us (2%)
    unnamed x22, waiting for transfers between devices  195 us
    all_gather x4, waiting for transfers between devices, gather_full(): return lax.all_gather(column, 'rep', axis=0, tiled=False)  183 us
    all_gather x3, waiting for transfers between devices, gather_full(): column = lax.all_gather(piece, 'shard', axis=0, tiled=True)  64 us
    unnamed x108, local copies, waits for them, and re-layouts  59.1 us
    reduce_scatter x2, waiting for transfers between devices, reduce_full(): part = lax.psum_scatter(part, 'shard', scatter_dimension=0, tiled=True)  50.8 us
    all_gather x3, blocking collectives, reduce_full(): pieces = lax.all_gather(part, 'rep', axis=0, tiled=False)  35.9 us
    dot_general x1, matrix products, attend_backward(): jnp.einsum('hqk,khd->qhd', score_grad, rotated_keys, preferred_element_ty...  26.2 us
    dot_general x1, matrix products, attend_backward(): jnp.einsum('hqk,qhd->khd', score_grad, queries, preferred_element_type=jn...  26.1 us
  transfers between devices with their start and end apart: 16, of which 15 were waited for; matrix products, arithmetic and copies ran while one was open for 31% of the time, Pallas kernels for 0%

profile of v1, /device:TPU:0, one launch (start us, length us, event | category | flops | bytes accessed | tf_op | source)
XLA Modules:
  0.0 931.1 jit_solution(1859404770817627660)
XLA Ops:
  16.7 19.5 %all_gather.63 = bf16[1024,256]{1,0:T(8,128)(2,1)} all-gather(bf16[128,256]{1,0:T(8,128)(2,1)S(1)} %dynamic-slice_convert_fusion.1), channel_id=1, replica_groups=mesh['rep'=4,'shard'=8] {'shard'}, dimensions={0}, use_global_device_ids=true | all-gather | bytes 589824 | tf_op jit(solution)/shard_map/all_gather | solution.py:109
  43.8 37.6 %all-gather.19.cloned.1.call-done = bf16[1024,1408]{1,0:T(8,128)(2,1)} async-done(((bf16[128,1408]{1,0:T(8,128)(2,1)}), bf16[1024,1408]{1,0:T(8,128)(2,1)}) %all-gather.19.cloned.1.call-update) | async-done | bytes 2883600 | tf_op jit(solution)/shard_map/all_gather | solution.py:109
  88.0 18.9 %all-gather.21.cloned.1.call-done = bf16[2816,256]{1,0:T(8,128)(2,1)} async-done(((bf16[352,256]{1,0:T(8,128)(2,1)}), bf16[2816,256]{1,0:T(8,128)(2,1)}) %all-gather.21.cloned.1.call-update) | async-done | bytes 1441808 | tf_op jit(solution)/shard_map/all_gather | solution.py:109
  107.5 36.0 %all-gather.25.cloned.1.call-done = bf16[4096,256]{1,0:T(8,128)(2,1)} async-done(((bf16[1024,256]{1,0:T(8,128)(2,1)}), bf16[4096,256]{1,0:T(8,128)(2,1)}) %all-gather.25.cloned.1.call-update) | async-done | bytes 2097168 | tf_op jit(solution)/shard_map/all_gather | solution.py:110
  147.4 67.9 %all-gather.23.cloned.1.call-done = bf16[4096,768]{0,1:T(8,128)(2,1)} async-done(((bf16[1024,768]{0,1:T(8,128)(2,1)}), bf16[4096,768]{0,1:T(8,128)(2,1)}) %all-gather.23.cloned.1.call-update) | async-done | bytes 6291472 | tf_op jit(solution)/shard_map/all_gather | solution.py:110
  263.5 10.3 %fusion.4 = f32[16,512]{1,0:T(8,128)S(1)} fusion(f32[16,512,512]{1,2,0:T(8,128)} %get-tuple-element.181, f32[16,512]{1,0:T(8,128)S(1)} %get-tuple-element.180), kind=kLoop, calls=%fused_computation.8 | loop fusion | flops 8380416 | bytes 16842752 | tf_op jit(solution)/shard_map/while/body/eval_jaxpr/reduce_sum | solution.py:59
  284.8 46.0 %all-gather.27.cloned.1.call-done = bf16[4096,1408]{1,0:T(8,128)(2,1)} async-done(((bf16[1024,1408]{1,0:T(8,128)(2,1)}), bf16[4096,1408]{1,0:T(8,128)(2,1)}) %all-gather.27.cloned.1.call-update) | async-done | bytes 11534352 | tf_op jit(solution)/shard_map/all_gather | solution.py:110
  330.9 12.5 %fusion.79 = f32[512,4,1408]{0,2,1:T(8,128)} fusion(bf16[4,1024,1408]{2,1,0:T(8,128)(2,1)} %bitcast.296, f32[512,1024]{1,0:T(8,128)} %copy-done.7, f32[512]{0:T(512)S(1)} %add_rsqrt_fusion, f32[512]{0:T(512)S(1)} %broadcast_multiply_fusion.4), kind=kOutput, calls=%fused_computation.134 | convolution fusion | flops 5907152896 | bytes 25169920 | tf_op jit(solution)/shard_map/rd,qdf->rqf/dot_general | solution.py:183
  343.4 9.9 %fusion.97 = (f32[512,1,2816]{0,2,1:T(8,128)}, f32[512,1,2816]{0,2,1:T(8,128)}) fusion(f32[512,2,2816]{0,2,1:T(8,128)} %bitcast.256), kind=kLoop, calls=%fused_computation.157 | loop fusion | bytes 23068672 | tf_op jit(solution)/shard_map/slice | solution.py:186
  365.9 32.7 %all-gather.29.cloned.1.call-done = bf16[11264,256]{1,0:T(8,128)(2,1)} async-done(((bf16[2816,256]{1,0:T(8,128)(2,1)}), bf16[11264,256]{1,0:T(8,128)(2,1)}) %all-gather.29.cloned.1.call-update) | async-done | bytes 5767184 | tf_op jit(solution)/shard_map/all_gather | solution.py:110
  398.5 11.1 %fusion.25 = (bf16[512,2816]{1,0:T(8,128)(2,1)S(1)}, bf16[512,2816]{1,0:T(8,128)(2,1)S(1)}) fusion(f32[512,1,2816]{2,0,1:T(8,128)} %copy.240, f32[512,1,2816]{2,0,1:T(8,128)} %copy.241, bf16[4,2816,256]{2,1,0:T(8,128)(2,1)} %bitcast.263, f32[512,4,256]{2,1,0:T(4,128)} %reshape.396, f32[512]{0:T(512)S(1)} %fusion.87), kind=kOutput, calls=%fused_computation.30 | convolution fusion | flops 2972581888 | bytes 25167872 | tf_op jit(solution)/shard_map/rqe,qfe->rf/dot_general | solution.py:196
  414.0 11.1 %bitcast_reduce_fusion.1 = (f32[512]{0:T(512)S(1)}, f32[512]{0:T(512)S(1)}, f32[512,1024,1]{1,0,2:T(8,128)S(1)}) fusion(f32[512]{0:T(512)S(1)} %add_rsqrt_fusion, f32[512,1024]{1,0:T(8,128)S(1)} %copy-done.8, f32[512]{0:T(512)S(1)} %broadcast_multiply_fusion.4, bf16[512,4,1408]{2,0,1:T(8,128)(2,1)} %bitcast_dynamic-update-slice_fusion, ...), kind=kOutput, calls=%fused_computation.81 | convolution fusion | flops 5908200448 | bytes 21504000 | tf_op jit(solution)/shard_map/rqf,qdf->rd/dot_general | solution.py:209
  432.8 12.2 %fusion.6 = bf16[4,1024,1408]{1,2,0:T(8,128)(2,1)} fusion(bf16[512,4,1408]{2,0,1:T(8,128)(2,1)} %bitcast_dynamic-update-slice_fusion, f32[512,1024]{1,0:T(8,128)} %copy-done.7, f32[512]{0:T(512)S(1)} %add_rsqrt_fusion, f32[512]{0:T(512)S(1)} %broadcast_multiply_fusion.4), kind=kOutput, calls=%fused_computation.11 | convolution fusion | flops 5912920064 | bytes 19402752 | tf_op jit(solution)/shard_map/rc,rqf->qcf/dot_general | solution.py:222
  474.0 26.2 %fusion.16 = f32[16,64,512]{2,1,0:T(8,128)} fusion(bf16[512,16,64]{0,2,1:T(8,128)(2,1)} %copy-done.22, f32[16,512,512]{1,2,0:T(8,128)} %fusion.101, f32[16,512,512]{1,2,0:T(8,128)} %get-tuple-element.181, f32[16,512]{1,0:T(8,128)S(1)} %log_add_fusion), kind=kOutput, calls=%fused_computation.19 | convolution fusion | flops 566239744 | bytes 36732928 | tf_op jit(solution)/shard_map/while/body/eval_jaxpr/hqk,khd->qhd/dot_general | solution.py:85
  503.8 26.1 %fusion.13 = f32[16,64,512]{2,1,0:T(8,128)} fusion(bf16[512,16,64]{0,2,1:T(8,128)(2,1)S(1)} %copy-done.21, f32[16,512,512]{1,2,0:T(8,128)} %fusion.101, f32[16,512,512]{1,2,0:T(8,128)} %get-tuple-element.181, f32[16,512]{1,0:T(8,128)S(1)} %log_add_fusion), kind=kOutput, calls=%fused_computation.18 | convolution fusion | flops 566239744 | bytes 36732928 | tf_op jit(solution)/shard_map/while/body/eval_jaxpr/hqk,qhd->khd/dot_general | solution.py:88
  554.3 29.4 %reduce-scatter.37.cloned.1.call-done = bf16[1,1024,1408]{1,2,0:T(8,128)(2,1)} async-done(((bf16[4,1024,1408]{1,2,0:T(8,128)(2,1)}), bf16[1,1024,1408]{1,2,0:T(8,128)(2,1)}) %reduce-scatter.37.cloned.1.call-update) | async-done | bytes 2883600
  588.3 64.4 %reduce-scatter.39.cloned.1.call-done = bf16[1,2816,256]{1,2,0:T(8,128)(2,1)} async-done(((bf16[4,2816,256]{1,2,0:T(8,128)(2,1)}), bf16[1,2816,256]{1,2,0:T(8,128)(2,1)}) %reduce-scatter.39.cloned.1.call-update) | async-done | bytes 1441808
  655.2 70.9 %reduce-scatter.33.cloned.1.call-done = bf16[1,1024,768]{1,2,0:T(8,128)(2,1)} async-done(((bf16[4,1024,768]{1,2,0:T(8,128)(2,1)}), bf16[1,1024,768]{1,2,0:T(8,128)(2,1)}) %reduce-scatter.33.cloned.1.call-update) | async-done | bytes 1572880
  770.9 28.9 %reduce-scatter.29.cloned.1.call-done = bf16[128,1408]{1,0:T(8,128)(2,1)} async-done(((bf16[1024,1408]{1,0:T(8,128)(2,1)}), bf16[128,1408]{1,0:T(8,128)(2,1)}) %reduce-scatter.29.cloned.1.call-update) | async-done | bytes 360464
  803.1 32.6 %reduce-scatter.31.cloned.1.call-done = bf16[352,256]{1,0:T(8,128)(2,1)} async-done(((bf16[2816,256]{1,0:T(8,128)(2,1)}), bf16[352,256]{1,0:T(8,128)(2,1)}) %reduce-scatter.31.cloned.1.call-update) | async-done | bytes 180240 | tf_op jit(solution)/shard_map/reduce_scatter | solution.py:115
  835.7 11.3 %all-gather.7 = bf16[1408,256]{1,0:T(8,128)(2,1)S(1)} all-gather(bf16[352,256]{1,0:T(8,128)(2,1)} %reduce-scatter.31.cloned.1.call-done), channel_id=9, replica_groups=mesh['rep'=4,'shard'=8] {'rep'}, dimensions={0}, use_global_device_ids=true | all-gather | bytes 901120 | tf_op jit(solution)/shard_map/all_gather | solution.py:116
  852.7 18.2 %reduce-scatter.25.cloned.1.call-done = bf16[128,768]{1,0:T(8,128)(2,1)} async-done(((bf16[1024,768]{1,0:T(8,128)(2,1)}), bf16[128,768]{1,0:T(8,128)(2,1)}) %reduce-scatter.25.cloned.1.call-update) | async-done | bytes 196624 | tf_op jit(solution)/shard_map/reduce_scatter | solution.py:115
  870.9 15.1 %all-gather.4 = bf16[512,768]{1,0:T(8,128)(2,1)S(1)} all-gather(bf16[128,768]{1,0:T(8,128)(2,1)} %reduce-scatter.25.cloned.1.call-done), channel_id=6, replica_groups=mesh['rep'=4,'shard'=8] {'rep'}, dimensions={0}, use_global_device_ids=true | all-gather | bytes 983040 | tf_op jit(solution)/shard_map/all_gather | solution.py:116
  912.2 12.2 %multiply_subtract_fusion = (f32[128,2,2816]{2,1,0:T(2,128)}, f32[128,2,2816]{2,1,0:T(2,128)}, f32[128,2,2816]{2,1,0:T(2,128)}) fusion(f32[128,2,2816]{2,1,0:T(2,128)S(1)} %copy-done.3, f32[]{:T(128)} %bitcast.61, f32[]{:T(128)} %bitcast.60, f32[]{:T(128)} %bitcast.246, f32[128,2,2816]{2,1,0:T(2,128)} %reshape.404, f32[128,2,2816]{2,1,0:T(2,128)} %param.32, ...), kind=kLoop, calls=%fused_computation.45 | loop fusion | flops 10813440 | bytes 20185100 | tf_op jit(solution)/shard_map/sub | solution.py:98
  (218 shorter events, 253.2 us)
Async XLA Ops:
  7.2 36.6 %all-gather.17.cloned.1.call-start = ((), (), s32[]{:S(2)}) async-start(), calls=%async_computation.8 | async-start | bytes 1769472 | tf_op jit(solution)/shard_map/all_gather | solution.py:109
  10.1 71.3 %all-gather.19.cloned.1.call-start = ((), (), s32[]{:S(2)}) async-start(), calls=%async_computation.9 | async-start | bytes 3244032 | tf_op jit(solution)/shard_map/all_gather | solution.py:109
  14.0 92.9 %all-gather.21.cloned.1.call-start = ((), (), s32[]{:S(2)}) async-start(), calls=%async_computation.10 | async-start | bytes 1622016 | tf_op jit(solution)/shard_map/all_gather | solution.py:109
  15.7 127.7 %all-gather.25.cloned.1.call-start = ((), (), s32[]{:S(2)}) async-start(), calls=%async_computation.12 | async-start | bytes 2621440 | tf_op jit(solution)/shard_map/all_gather | solution.py:110
  36.2 179.1 %all-gather.23.cloned.1.call-start = ((), (), s32[]{:S(2)}) async-start(), calls=%async_computation.11 | async-start | bytes 7864320 | tf_op jit(solution)/shard_map/all_gather | solution.py:110
  43.7 38.5 %copy-start.4 = (bf16[1,512,1024]{2,1,0:T(8,128)(2,1)S(1)}, bf16[1,512,1024]{2,1,0:T(8,128)(2,1)}, u32[]{:S(2)}) copy-start(bf16[1,512,1024]{2,1,0:T(8,128)(2,1)} %param.19) | copy-start | bytes 3145732
  43.8 287.1 %all-gather.27.cloned.1.call-start = ((), (), s32[]{:S(2)}) async-start(), calls=%async_computation.13 | async-start | bytes 14417920 | tf_op jit(solution)/shard_map/all_gather | solution.py:110
  81.5 317.1 %all-gather.29.cloned.1.call-start = ((), (), s32[]{:S(2)}) async-start(), calls=%async_computation.14 | async-start | bytes 7208960 | tf_op jit(solution)/shard_map/all_gather | solution.py:110
  87.4 145.6 %copy-start.39 = (f32[512]{0:T(512)}, f32[512]{0:T(512)S(1)}, u32[]{:S(2)}) copy-start(f32[512]{0:T(512)S(1)} %broadcast_multiply_fusion.5) | copy-start | bytes 6148
  87.8 145.2 %copy-start.41 = (f32[512]{0:T(512)}, f32[512]{0:T(512)S(1)}, u32[]{:S(2)}) copy-start(f32[512]{0:T(512)S(1)} %add_rsqrt_fusion.1) | copy-start | bytes 6148
  106.9 445.2 %reduce-scatter.35.cloned.1.call-start = ((), (), s32[]{:S(2)}) async-start(), calls=%async_computation.21 | async-start | bytes 2621440
  432.7 150.9 %reduce-scatter.37.cloned.1.call-start = ((), (), s32[]{:S(2)}) async-start(), calls=%async_computation.22 | async-start | bytes 14417920
  445.0 207.7 %reduce-scatter.39.cloned.1.call-start = ((), (), s32[]{:S(2)}) async-start(), calls=%async_computation.23 | async-start | bytes 7208960
  458.7 267.4 %reduce-scatter.33.cloned.1.call-start = ((), (), s32[]{:S(2)}) async-start(), calls=%async_computation.20 | async-start | bytes 7864320
  503.8 28.1 %copy-start.33 = (f32[512,64]{0,1:T(8,128)S(1)}, f32[512,64]{0,1:T(8,128)}, u32[]{:S(2)}) copy-start(f32[512,64]{0,1:T(8,128)} %get-tuple-element.177) | copy-start | bytes 393220
  551.9 208.0 %reduce-scatter.27.cloned.1.call-start = ((), (), s32[]{:S(2)}) async-start(), calls=%async_computation.17 | async-start | bytes 589824
  554.2 245.5 %reduce-scatter.29.cloned.1.call-start = ((), (), s32[]{:S(2)}) async-start(), calls=%async_computation.18 | async-start | bytes 3244032
  588.2 247.5 %reduce-scatter.31.cloned.1.call-start = ((), (), s32[]{:S(2)}) async-start(), calls=%async_computation.19 | async-start | bytes 1622016 | tf_op jit(solution)/shard_map/reduce_scatter | solution.py:115
  655.2 215.7 %reduce-scatter.25.cloned.1.call-start = ((), (), s32[]{:S(2)}) async-start(), calls=%async_computation.16 | async-start | bytes 1769472 | tf_op jit(solution)/shard_map/reduce_scatter | solution.py:115
  728.7 172.2 %all-gather.31.cloned.1.call-start = ((), (), s32[]{:S(2)}) async-start(), calls=%async_computation.15 | async-start | bytes 1802240 | tf_op jit(solution)/shard_map/all_gather | solution.py:116
  760.8 40.9 %copy-start.32 = (f32[128,1024]{1,0:T(8,128)S(1)}, f32[128,1024]{1,0:T(8,128)}, u32[]{:S(2)}) copy-start(f32[128,1024]{1,0:T(8,128)} %param.27) | copy-start | bytes 1572868
  760.8 40.9 %copy-start.35 = (f32[128,1024]{1,0:T(8,128)S(1)}, f32[128,1024]{1,0:T(8,128)}, u32[]{:S(2)}) copy-start(f32[128,1024]{1,0:T(8,128)} %param.29) | copy-start | bytes 1572868
  760.9 40.9 %copy-start.36 = (f32[128,1024]{1,0:T(8,128)S(1)}, f32[128,1024]{1,0:T(8,128)}, u32[]{:S(2)}) copy-start(f32[128,1024]{1,0:T(8,128)} %param.28) | copy-start | bytes 1572868
  770.8 32.3 %copy-start.27 = (f32[16,8,4,256]{3,1,2,0:T(8,128)}, f32[16,8,4,256]{3,1,2,0:T(8,128)S(1)}, u32[]{:S(2)}) copy-start(f32[16,8,4,256]{3,1,2,0:T(8,128)S(1)} %copy.247) | copy-start | bytes 1572868
  (37 other events, 137.6 us)
Sparse Core Ops, SparseCore 0:
  10.3 33.4 all-gather.16
  46.0 35.4 all-gather.18
  83.6 23.2 all-gather.20
  108.6 34.8 all-gather.24
  145.1 70.1 all-gather.22
  217.0 113.7 all-gather.26
  332.7 65.7 all-gather.28
  432.9 35.1 reduce-scatter.34
  471.5 112.1 reduce-scatter.36
  586.8 65.8 reduce-scatter.38
  655.9 70.1 reduce-scatter.32
  728.9 30.9 reduce-scatter.26
  762.8 36.9 reduce-scatter.28
  802.5 33.1 reduce-scatter.30
  838.4 32.4 reduce-scatter.24
  873.2 27.6 all-gather.30

commit v2 on v1

--- a/solution.py
+++ b/solution.py
@@ -1,7 +1,15 @@
+import functools
+
 import jax
 import jax.numpy as jnp
 from jax import lax
+from jax.experimental import pallas as pl
+from jax.experimental.pallas import tpu as pltpu
 from jax.sharding import PartitionSpec as P
+
+MESH = pl.DeviceIdType.MESH
+DMA = pltpu.SemaphoreType.DMA
+RING = 4
 
 HD = 64
 
@@ -101,6 +109,393 @@
     return (gradient, weight_new, first_new, second_new)
 
 
+class Gather:
+    NSEM = 9
+    @staticmethod
+    def scratch(nt, nc):
+        return [DMA((nt,)), DMA((nc, 4)), DMA((nc, 4)), DMA((nc, 2, 3)), DMA((nc, 2, 3)), DMA((nc, 3, 2)), DMA((nc, 3, 2)), DMA((nc, 3, 2)), DMA((nc, 3, 2))]
+    def __init__(self, shapes, chunks, loc, full, sems):
+        self.shapes, self.chunks, self.loc, self.full = shapes, chunks, loc, full
+        (self.cp, self.sib_s, self.sib_r, self.z_s, self.z_r, self.p_s, self.p_r, self.d_s, self.d_r) = sems
+        self.rep = lax.axis_index("rep"); self.shard = lax.axis_index("shard")
+        self.z = self.shard // 2; self.core = lax.rem(self.shard, 2)
+        self.x = lax.rem(self.rep, 2); self.y = self.rep // 2
+        self.sib = (self.rep, self.shard + 1 - 2 * self.core)
+        self.nb = ((self.rep + 1 - 2 * self.x, self.shard), (self.rep + 2 - 4 * self.y, self.shard))
+        self.diag = self.rep + (1 - 2 * self.x) + (2 - 4 * self.y)
+    def barrier(self):
+        bar = pltpu.get_barrier_semaphore()
+        for dev in (self.sib,) + self.nb + tuple((self.rep, lax.rem(self.shard + 2 * d, 8)) for d in (1, 2, 3)):
+            pl.semaphore_signal(bar, inc=1, device_id=dev, device_id_type=MESH)
+        pl.semaphore_wait(bar, 6)
+    def ref(self, c, s, q=None, half=None):
+        t, r0, rows, c0, cols, axis = self.chunks[c]
+        R = self.shapes[t][0]
+        ro, co, nr, ncl = r0, c0, rows, cols
+        base = s * R + r0
+        if q is not None:
+            parts, i = (4, q) if half is None else (8, 2 * q + half)
+            if axis == 0:
+                nr = rows // parts; base = base + i * nr
+            else:
+                ncl = cols // parts; co = pl.multiple_of(c0 + i * ncl, 128)
+        base = pl.multiple_of(base, 16 if nr % 16 == 0 else 8)
+        return self.full[t].at[pl.ds(base, nr), pl.ds(co, ncl)]
+    def loc_ref(self, c, q=None):
+        t, r0, rows, c0, cols, axis = self.chunks[c]
+        nr, ncl, ro, co = rows, cols, r0, c0
+        if q is not None:
+            if axis == 0: nr = rows // 4; ro = pl.multiple_of(r0 + q * nr, 16)
+            else: ncl = cols // 4; co = pl.multiple_of(c0 + q * ncl, 128)
+        return self.loc[t].at[pl.ds(ro, nr), pl.ds(co, ncl)]
+    def rc(self, src, dst, ss, rs, dev):
+        return pltpu.make_async_remote_copy(src_ref=src, dst_ref=dst, send_sem=ss, recv_sem=rs, device_id=dev, device_id_type=MESH)
+    def own(self, t):
+        R, C, = self.shapes[t]
+        return pltpu.make_async_copy(self.loc[t], self.full[t].at[pl.ds(pl.multiple_of(self.shard * R, R), R), :], self.cp.at[t])
+    def other(self, dz): return lax.rem(self.shard + 2 * dz, 8)
+    def sibc(self, c, dz):
+        r = self.ref(c, self.other(dz))
+        return self.rc(self.loc_ref(c) if dz == 0 else r, r, self.sib_s.at[c, dz], self.sib_r.at[c, dz], self.sib)
+    def zc(self, c, side, h, first):
+        sgn = 1 if side == 0 else -1
+        s = self.shard - sgn * 2 * (h - 1)
+        src = self.loc_ref(c, self.rep) if first else self.ref(c, s, self.rep)
+        return self.rc(src, self.ref(c, s, self.rep), self.z_s.at[c, side, h - 1], self.z_r.at[c, side, h - 1], (self.rep, self.shard + sgn * 2))
+    def z_send(self, c, side, h):
+        can = (self.z < 3) if side == 0 else (self.z > 0)
+        has = (self.z >= h - 1) if side == 0 else (self.z <= 3 - (h - 1))
+        return jnp.logical_and(can, has)
+    def z_got(self, side, h):
+        return (self.z >= h) if side == 0 else (self.z <= 3 - h)
+    def zr(self, c, side, h):
+        sgn = 1 if side == 0 else -1
+        s = self.shard - sgn * 2 * h
+        r = self.ref(c, s, self.rep)
+        return self.rc(r, r, self.z_s.at[c, side, h - 1], self.z_r.at[c, side, h - 1], (self.rep, self.shard - sgn * 2))
+    def pc(self, c, dz, k, q=None):
+        q = self.rep if q is None else q
+        r = self.ref(c, self.other(dz), q)
+        return self.rc(r, r, self.p_s.at[c, dz - 1, k], self.p_r.at[c, dz - 1, k], self.nb[k])
+    def dc(self, c, dz, k, q=None):
+        q = self.nb[k][0] if q is None else q
+        r = self.ref(c, self.other(dz), q, k)
+        return self.rc(r, r, self.d_s.at[c, dz - 1, k], self.d_r.at[c, dz - 1, k], self.nb[1 - k])
+    def s0(self, c):
+        for side in (0, 1):
+            @pl.when(self.z_send(c, side, 1))
+            def _(): self.zc(c, side, 1, True).start()
+        self.sibc(c, 0).start()
+    def s1(self, c, h):
+        for side in (0, 1):
+            @pl.when(self.z_got(side, h))
+            def _():
+                self.zr(c, side, h).wait_recv()
+                if h < 3:
+                    @pl.when((self.z < 3) if side == 0 else (self.z > 0))
+                    def _(): self.zc(c, side, h + 1, False).start()
+                dz = (4 - h) if side == 0 else h
+                for k in (0, 1): self.pc(c, dz, k).start()
+    def order(self):
+        return (1, 3, 2)
+    def s2(self, c):
+        for dz in self.order():
+            for k in (0, 1):
+                self.pc(c, dz, k, self.nb[k][0]).wait_recv(); self.dc(c, dz, k).start()
+    def s3(self, c):
+        for dz in self.order():
+            for k in (0, 1): self.dc(c, dz, k, self.diag).wait_recv()
+            self.sibc(c, dz).start()
+    def done(self, c):
+        for dz in range(4): self.sibc(c, dz).wait()
+    def drain(self, c):
+        for side in (0, 1):
+            for h in (1, 2, 3):
+                @pl.when(self.z_send(c, side, h))
+                def _(): self.zc(c, side, h, h == 1).wait_send()
+        for dz in (1, 2, 3):
+            for k in (0, 1): self.pc(c, dz, k).wait_send(); self.dc(c, dz, k).wait_send()
+
+def gather_kernel(shapes, chunks, lags, *refs):
+    n = len(shapes); nc = len(chunks)
+    g = Gather(shapes, chunks, refs[:n], refs[n:2 * n], refs[2 * n:])
+    g.barrier()
+    for t in range(n): g.own(t).start()
+    stages = [g.s0] + [functools.partial(lambda h, c: g.s1(c, h), h) for h in (1, 2, 3)] + [g.s2, g.s3, g.done]
+    for i in range(nc + max(lags)):
+        for st, lag in zip(stages, lags):
+            if 0 <= i - lag < nc: st(i - lag)
+    for t in range(n): g.own(t).wait()
+    for c in range(nc): g.drain(c)
+
+def gather_call(locs):
+    shapes = [l.shape for l in locs]
+    rows, qkv = shapes[0]
+    gate_up = shapes[2][1] // 2
+    chunks = (
+        (0, 0, rows, 0, qkv, 1),
+        (1, 0, rows, 0, shapes[1][1], 1),
+        (2, 0, rows, 0, gate_up, 0),
+        (2, 0, rows, gate_up, gate_up, 0),
+        (3, 0, shapes[3][0], 0, shapes[3][1], 1),
+    )
+    lags = (0, 1, 2, 3, 3, 4, 5)
+    n, nc = len(shapes), len(chunks)
+    return pl.pallas_call(functools.partial(gather_kernel, shapes, chunks, lags),
+        out_shape=[jax.ShapeDtypeStruct((8 * r, c), jnp.bfloat16) for r, c in shapes],
+        in_specs=[pl.BlockSpec(memory_space=pl.ANY)] * n, out_specs=[pl.BlockSpec(memory_space=pl.ANY)] * n,
+        scratch_shapes=Gather.scratch(n, nc),
+        compiler_params=pltpu.CompilerParams(collective_id=0, has_side_effects=True))(*locs)
+
+class Reduce:
+    def __init__(self, refs):
+        (self.mine, self.theirs, self.held, self.got, self.sums, self.one, self.two, self.fin, self.planes, self.total,
+         self.a_s, self.a_r, self.o_s, self.o_r, self.t_s, self.t_r, self.c_s, self.c_r, self.d_s, self.d_r, self.f_s, self.f_r) = refs
+        self.rep, self.shard = lax.axis_index("rep"), lax.axis_index("shard")
+        self.core = lax.rem(self.shard, 2)
+        self.x, self.y = lax.rem(self.rep, 2), self.rep // 2
+        self.sib = (self.rep, self.shard + 1 - 2 * self.core)
+        self.nb = ((self.rep + 1 - 2 * self.x, self.shard), (self.rep + 2 - 4 * self.y, self.shard))
+
+    @staticmethod
+    def scratch(chunks, wide):
+        v = lambda *s: pltpu.VMEM(s, jnp.bfloat16)
+        return [
+            v(RING, 8, 16, wide),
+            v(RING, 8, 16, wide),
+            pltpu.VMEM((2, 8, 16, wide), jnp.float32),
+            None, v(RING, 8, 16, wide),
+            v(2, RING, 2, 16, wide),
+            v(2, RING, 16, wide),
+            v(RING, 2, 16, wide),
+            v(chunks, 3, 2, 16, wide),
+            None,
+        ], [DMA((RING,)), DMA((RING,)), DMA((2, RING)), DMA((2, RING)), DMA((2, RING)), DMA((2, RING)), DMA((RING,)), DMA((chunks, 3)),
+            DMA((chunks, 2)), DMA((chunks, 2)), DMA((chunks, 2)), DMA((chunks, 2))]
+
+    def copy(self, src, dst, s, r, dev):
+        return pltpu.make_async_remote_copy(src_ref=src, dst_ref=dst, send_sem=s, recv_sem=r, device_id=dev, device_id_type=MESH)
+
+    def barrier(self):
+        bar = pltpu.get_barrier_semaphore()
+        for dev in (self.sib,) + self.nb + tuple((self.rep, lax.rem(self.shard + 2 * d, 8)) for d in (1, 2, 3)):
+            pl.semaphore_signal(bar, inc=1, device_id=dev, device_id_type=MESH)
+        pl.semaphore_wait(bar, 6)
+
+    def first(self, u, w):
+        s = lax.rem(u, RING)
+        return self.copy(self.mine.at[s, :, :, pl.ds(0, w)], self.theirs.at[s, :, :, pl.ds(0, w)], self.a_s.at[s], self.a_r.at[s], self.sib)
+
+    def hop_one(self, u, w, k):
+        s = lax.rem(u, RING)
+        at = 2 - 2 * self.x if k == 0 else 6 - 2 * self.y
+        return self.copy(self.sums.at[s, pl.ds(at, 2), :, pl.ds(0, w)], self.one.at[k, s, :, :, pl.ds(0, w)], self.o_s.at[k, s], self.o_r.at[k, s], self.nb[k])
+
+    def hop_two(self, u, w, k):
+        s = lax.rem(u, RING)
+        at = 2 * self.x + 1 - self.y if k == 0 else 4 + 2 * self.y + 1 - self.x
+        return self.copy(self.sums.at[s, at, :, pl.ds(0, w)], self.two.at[k, s, :, pl.ds(0, w)], self.t_s.at[k, s], self.t_r.at[k, s], self.nb[1 - k])
+
+    def across(self, u, w, dz):
+        s = lax.rem(u, RING)
+        c = u // 4
+        return self.copy(self.fin.at[s, :, :, pl.ds(0, w)], self.planes.at[c, 3 - dz, :, :, pl.ds(0, w)], self.c_s.at[s], self.c_r.at[c, 3 - dz], (self.rep, lax.rem(self.shard + 2 * dz, 8)))
+
+    def plane_in(self, c, w, j):
+        return self.copy(self.fin.at[0, :, :, pl.ds(0, w)], self.planes.at[c, j, :, :, pl.ds(0, w)], self.c_s.at[0], self.c_r.at[c, j], self.sib)
+
+    def spread(self, c, w, k, own=True):
+        q = self.rep if own else self.nb[k][0]
+        ref = self.total.at[c, q, :, :, pl.ds(0, w)]
+        return self.copy(ref, ref, self.d_s.at[c, k], self.d_r.at[c, k], self.nb[k])
+
+    def spread_on(self, c, w, k, own=True):
+        q = self.nb[k][0] if own else self.nb[0][0] + self.nb[1][0] - self.rep
+        ref = self.total.at[c, q, k, :, pl.ds(0, w)]
+        return self.copy(ref, ref, self.f_s.at[c, k], self.f_r.at[c, k], self.nb[1 - k])
+
+    def stage_two(self, u, w):
+        s = lax.rem(u, RING)
+        self.first(u, w).wait()
+        self.sums[s, :, :, :w] = (self.held[lax.rem(u, 2), :, :, :w] + self.theirs[s, :, :, :w].astype(jnp.float32)).astype(jnp.bfloat16)
+        for k in (0, 1):
+            self.hop_one(u, w, k).start()
+
+    def stage_three(self, u, w):
+        s = lax.rem(u, RING)
+        for k in (0, 1):
+            self.hop_one(u, w, k).wait()
+            at = 2 * self.x if k == 0 else 4 + 2 * self.y
+            new = self.sums[s, pl.ds(at, 2), :, :w].astype(jnp.float32) + self.one[k, s, :, :, :w].astype(jnp.float32)
+            self.sums[s, pl.ds(at, 2), :, :w] = new.astype(jnp.bfloat16)
+            self.hop_two(u, w, k).start()
+
+    def stage_four(self, u, w, start):
+        s = lax.rem(u, RING)
+        c = u // 4
+        dz = lax.rem(lax.rem(u, 4) + 1, 4)
+
+        @pl.when(jnp.logical_and(u >= start + RING, dz > 0))
+        def _():
+            self.across(u - RING, w, dz).wait_send()
+
+        for k in (0, 1):
+            self.hop_two(u, w, k).wait()
+
+        def plane_sum(k):
+            at = 2 * self.x + self.y if k == 0 else 4 + 2 * self.y + self.x
+            return self.sums[s, at, :, :w].astype(jnp.float32) + self.two[k, s, :, :w].astype(jnp.float32)
+
+        @pl.when(dz > 0)
+        def _():
+            for k in (0, 1):
+                self.fin[s, k, :, :w] = plane_sum(k).astype(jnp.bfloat16)
+            self.across(u, w, dz).start()
+
+        @pl.when(dz == 0)
+        def _():
+            for j in range(3):
+                self.plane_in(c, w, j).wait_recv()
+            for k in (0, 1):
+                out = plane_sum(k)
+                for j in range(3):
+                    out = out + self.planes[c, j, k, :, :w].astype(jnp.float32)
+                self.total[c, self.rep, k, :, :w] = out.astype(jnp.bfloat16)
+            for k in (0, 1):
+                self.spread(c, w, k).start()
+
+    def stage_five(self, u, w):
+        @pl.when(lax.rem(u, 4) == 3)
+        def _():
+            c = u // 4
+            for k in (0, 1):
+                self.spread(c, w, k, False).wait_recv()
+                self.spread_on(c, w, k).start()
+
+    def drain_across(self, units, w):
+        for u in range(units - RING, units):
+            if u % 4 != 3:
+                self.across(u, w, u % 4 + 1).wait_send()
+
+    def finish(self, units, width):
+        self.drain_across(units, width(units - 1))
+        for c in range(units // 4):
+            w = width(4 * c)
+            for k in (0, 1):
+                self.spread(c, w, k).wait_send()
+                self.spread_on(c, w, k).wait_send()
+                self.spread_on(c, w, k, False).wait_recv()
+
+
+def reduce_kernel(plan, wide, *refs):
+    left_ref, at_ref, at_r, gu_l, gu_r, dn_l, dn_r = (None,) + refs[:6]
+    total = refs[6]
+    s = refs[7:]
+    r = Reduce((s[0], s[1], s[2], None, s[3], s[4], s[5], s[6], s[7], total) + tuple(s[8:]))
+    units = 4 * sum(n for _, n, _ in plan)
+    bounds, u0 = [], 0
+    for kind, n, w in plan:
+        bounds.append((u0, u0 + 4 * n, kind, w))
+        u0 += 4 * n
+
+    def width(u):
+        for a, b, _, w in bounds:
+            if a <= u < b:
+                return w
+
+    def start_of(w):
+        return min(a for a, _, _, v in bounds if v == w)
+
+    def plane_of(u):
+        return lax.rem(r.shard // 2 + lax.rem(u, 4) + 1, 4)
+
+    def product(u, kind, first, own):
+        c = u // 4 - first // 4
+        zt = plane_of(u)
+        core = r.core if own else 1 - r.core
+        dst = (lambda e, lo, n, val: r.held.__setitem__((lax.rem(u, 2), e, slice(None), pl.ds(lo, n)), val)) if own else (
+            lambda e, lo, n, val: r.mine.__setitem__((lax.rem(u, RING), e, slice(None), pl.ds(lo, n)), val.astype(jnp.bfloat16)))
+        if kind == 0:
+            rows = dn_l.shape[0] // 8
+            part = rows // 2
+            base = pl.multiple_of((2 * zt + core) * rows + c * part, 16)
+            left = dn_l[pl.ds(base, part), :]
+            for e in range(8):
+                if e % 2 == 0:
+                    out = jnp.dot(left, dn_r[:, e * 128:e * 128 + 256], preferred_element_type=jnp.float32)
+                for j in range(part // 16):
+                    dst(e, 128 * j, 128, out[16 * j:16 * j + 16, (e % 2) * 128:(e % 2) * 128 + 128])
+        elif kind == 1:
+            base = pl.multiple_of((2 * zt + core) * 128, 128)
+            left = gu_l[pl.ds(base, 128), :]
+            col = pl.multiple_of(c * wide, 128)
+            out = jnp.dot(left, gu_r[:, pl.ds(col, wide)], preferred_element_type=jnp.float32)
+            dst(slice(None), 0, wide, out.reshape(8, 16, wide))
+        else:
+            n = 1024
+            base = pl.multiple_of((2 * zt + core) * 128 + jnp.where(c == 0, 1024, 0), 128)
+            left = at_ref[pl.ds(base, 128), :]
+            col = pl.multiple_of(c * n, 128)
+            out = jnp.dot(left, at_r[:, pl.ds(col, n)], preferred_element_type=jnp.float32)
+            dst(slice(None), 0, n, out.reshape(8, 16, n))
+
+    def step(u, kind, first, ws):
+        product(u, kind, first, False)
+        r.first(u, ws[0]).start()
+        product(u, kind, first, True)
+        tail(u, ws)
+
+    def tail(u, ws):
+        if ws[1]: r.stage_two(u - 1, ws[1])
+        if ws[2]: r.stage_three(u - 2, ws[2])
+        if ws[3]: r.stage_four(u - 3, ws[3], start_of(ws[3]))
+        if ws[4]: r.stage_five(u - 4, ws[4])
+
+    r.barrier()
+    for a, b, kind, w in bounds:
+        u = a
+        while u < b:
+            ws = [width(u - k) if u - k >= 0 else None for k in range(5)]
+            if all(x == w for x in ws):
+                lax.fori_loop(u, b, lambda i, _: (step(i, kind, a, ws), 0)[1], 0)
+                break
+            if u >= 4 and ws[3] and u - 4 >= 0 and u - 3 == start_of(ws[3]) and u - 3 > 0:
+                r.drain_across(u - 3, width(u - 4))
+            step(jnp.int32(u), kind, a, ws)
+            u += 1
+    for u in range(units, units + 4):
+        ws = [width(u - k) if 0 <= u - k < units else None for k in range(5)]
+        tail(jnp.int32(u), ws)
+    r.finish(units, width)
+
+
+def reduce_call(attn_left, attn_right, gu_left, gu_right, down_left, down_right):
+    wide = gu_right.shape[1] // 4
+    plan = ((0, 2, wide), (1, 4, wide), (2, 4, 1024))
+    vs, sems = Reduce.scratch(10, wide)
+    vm = pl.BlockSpec(memory_space=pltpu.VMEM)
+    return pl.pallas_call(
+        functools.partial(reduce_kernel, plan, wide),
+        out_shape=jax.ShapeDtypeStruct((10, 4, 2, 16, wide), jnp.bfloat16),
+        in_specs=[vm] * 6,
+        out_specs=vm,
+        scratch_shapes=[v for v in vs if v is not None] + sems,
+        compiler_params=pltpu.CompilerParams(collective_id=1, has_side_effects=True, vmem_limit_bytes=56 << 20),
+    )(attn_left, attn_right, gu_left, gu_right, down_left, down_right)
+
+
+def pieces(total, c, w):
+    t = total[c, :, :, :, :w]
+    return jnp.stack([t[0, 0], t[2, 0], t[1, 0], t[3, 0]] + [t[i, 1] for i in range(4)])
+
+
+def unpack(total, wide):
+    down = [pieces(total, c, wide).reshape(8, 16, wide // 128, 128).transpose(2, 1, 0, 3).reshape(-1, 1024) for c in (0, 1)]
+    gu = [pieces(total, c, wide).reshape(128, wide) for c in (2, 3, 4, 5)]
+    at = [pieces(total, c, 1024).reshape(128, 1024) for c in (6, 7, 8, 9)]
+    return jnp.concatenate(down, 0), jnp.concatenate(gu, 1), at[0], jnp.stack(at[1:], 1)
+
+
 def gather_full(local, rep_count, rep_index):
     rows = local.shape[0]
     flat = local.reshape(rows, -1)
@@ -118,7 +513,7 @@
     return jnp.transpose(pieces, (1, 0, 2)).reshape(rows, -1).astype(jnp.float32)
 
 
-def shards(
+def shards_generic(
     tokens,
     cotangent,
     lengths,
@@ -307,9 +702,168 @@
     )
 
 
+def shards_fast(
+    tokens,
+    cotangent,
+    lengths,
+    slot_sequence,
+    step_count,
+    learn_rate,
+    attention_in,
+    attention_in_first,
+    attention_in_second,
+    attention_out,
+    attention_out_first,
+    attention_out_second,
+    gate_up_weight,
+    gate_up_first,
+    gate_up_second,
+    down_weight,
+    down_first,
+    down_second,
+):
+    slot_count, position_count, feature_count = tokens.shape
+    row_total = slot_count * position_count
+    head_count = feature_count // HD
+    shaped = (slot_count, position_count, head_count, HD)
+    inputs = tokens.astype(jnp.float32).reshape(row_total, feature_count)
+    matches = jnp.arange(lengths.shape[0])[None, :] == slot_sequence[:, None]
+    slot_length = jnp.sum(jnp.where(matches, lengths[None, :], 0), axis=1)
+    alive_rows = (
+        (jnp.arange(position_count)[None, :] < slot_length[:, None])
+        .astype(jnp.float32)
+        .reshape(row_total, 1)
+    )
+    cosine_table, sine_table = rope_tables(position_count, HD)
+    in_local = attention_in.astype(jnp.bfloat16)
+    out_local = attention_out.astype(jnp.bfloat16)
+    gate_up_local = gate_up_weight.astype(jnp.bfloat16)
+    down_local = down_weight.astype(jnp.bfloat16)
+    locs = [
+        in_local.reshape(in_local.shape[0], -1),
+        out_local,
+        gate_up_local.reshape(gate_up_local.shape[0], -1),
+        down_local,
+    ]
+    in_full, out_full, gate_up_full, down_full = gather_call(locs)
+    normed_one, inverse_one = layer_norm(inputs)
+    first_input = normed_one.astype(jnp.bfloat16)
+    projected = jnp.dot(first_input, in_full, preferred_element_type=jnp.float32).reshape(
+        row_total, 3, feature_count
+    )
+    queries = rotate(projected[:, 0].reshape(shaped), cosine_table, sine_table).astype(jnp.bfloat16)
+    rotated_keys = rotate(projected[:, 1].reshape(shaped), cosine_table, sine_table).astype(
+        jnp.bfloat16
+    )
+    values_low = projected[:, 2].reshape(shaped).astype(jnp.bfloat16)
+    mixed_heads, log_total = lax.map(
+        attend_forward, (queries, rotated_keys, values_low, slot_length)
+    )
+    mixed_low = mixed_heads.reshape(row_total, feature_count).astype(jnp.bfloat16)
+    residual = inputs + jnp.dot(mixed_low, out_full, preferred_element_type=jnp.float32)
+    normed_two, inverse_two = layer_norm(residual)
+    second_input = normed_two.astype(jnp.bfloat16)
+    gate_up = jnp.dot(second_input, gate_up_full, preferred_element_type=jnp.float32)
+    hidden_count = down_full.shape[0]
+    gate_value = gate_up[:, :hidden_count]
+    up_value = gate_up[:, hidden_count:]
+    sigmoid_gate = jax.nn.sigmoid(gate_value)
+    hidden_low = (gate_value * sigmoid_gate * up_value).astype(jnp.bfloat16)
+    result = residual + jnp.dot(hidden_low, down_full, preferred_element_type=jnp.float32)
+    output = (result * alive_rows).astype(jnp.bfloat16).reshape(tokens.shape)
+    output_grad = cotangent.astype(jnp.float32).reshape(row_total, feature_count) * alive_rows
+    result_grad_low = output_grad.astype(jnp.bfloat16)
+    hidden_grad = jnp.einsum(
+        "re,fe->rf", result_grad_low, down_full, preferred_element_type=jnp.float32
+    )
+    gate_grad = hidden_grad * up_value * sigmoid_gate * (1.0 + gate_value * (1.0 - sigmoid_gate))
+    up_grad = hidden_grad * gate_value * sigmoid_gate
+    gate_up_grad_low = jnp.concatenate([gate_grad, up_grad], axis=1).astype(jnp.bfloat16)
+    second_input_grad = jnp.einsum(
+        "rf,df->rd", gate_up_grad_low, gate_up_full, preferred_element_type=jnp.float32
+    )
+    residual_grad = output_grad + norm_back(normed_two, inverse_two, second_input_grad)
+    branch_grad = residual_grad.astype(jnp.bfloat16)
+    mixed_grad = (
+        jnp.einsum("re,de->rd", branch_grad, out_full, preferred_element_type=jnp.float32)
+        .astype(jnp.bfloat16)
+        .reshape(shaped)
+    )
+    query_grad, key_grad, value_grad = lax.map(
+        attend_backward, (queries, rotated_keys, values_low, slot_length, log_total, mixed_grad)
+    )
+    query_back = rotate(query_grad, cosine_table, -sine_table).reshape(row_total, feature_count)
+    key_back = rotate(key_grad, cosine_table, -sine_table).reshape(row_total, feature_count)
+    projected_grad = (
+        jnp.concatenate([query_back, key_back, value_grad.reshape(row_total, feature_count)], axis=1)
+        .astype(jnp.bfloat16)
+    )
+    first_input_grad = jnp.einsum(
+        "re,de->rd", projected_grad, in_full, preferred_element_type=jnp.float32
+    )
+    input_grad = (residual_grad + norm_back(normed_one, inverse_one, first_input_grad)).reshape(
+        tokens.shape
+    )
+    total = reduce_call(
+        jnp.concatenate([first_input.T, mixed_low.T], axis=0),
+        jnp.concatenate([branch_grad, projected_grad], axis=1),
+        second_input.T,
+        gate_up_grad_low,
+        hidden_low.T,
+        result_grad_low,
+    )
+    down_part, gate_up_part, out_part, in_part = [
+        part.astype(jnp.float32) for part in unpack(total, 2 * hidden_count // 4)
+    ]
+    gate_up_part = gate_up_part.reshape(gate_up_weight.shape)
+    in_grad, in_new, in_first, in_second = adam_update(
+        attention_in,
+        attention_in_first,
+        attention_in_second,
+        in_part,
+        step_count,
+        learn_rate,
+    )
+    out_grad, out_new, out_first, out_second = adam_update(
+        attention_out,
+        attention_out_first,
+        attention_out_second,
+        out_part,
+        step_count,
+        learn_rate,
+    )
+    gu_grad, gu_new, gu_first, gu_second = adam_update(
+        gate_up_weight, gate_up_first, gate_up_second, gate_up_part, step_count, learn_rate
+    )
+    dn_grad, dn_new, dn_first, dn_second = adam_update(
+        down_weight, down_first, down_second, down_part, step_count, learn_rate
+    )
+    return (
+        output,
+        input_grad,
+        in_grad,
+        in_new,
+        in_first,
+        in_second,
+        out_grad,
+        out_new,
+        out_first,
+        out_second,
+        gu_grad,
+        gu_new,
+        gu_first,
+        gu_second,
+        dn_grad,
+        dn_new,
+        dn_first,
+        dn_second,
+    )
+
+
 def solution(mesh):
+    fast = mesh.shape["rep"] == 4 and mesh.shape["shard"] == 8
     return jax.shard_map(
-        shards,
+        shards_fast if fast else shards_generic,
         mesh=mesh,
         in_specs=(
             P(("rep", "shard"), None, None),

time: 937 us -> 543 us (0.58)
  waiting for transfers between devices: 493 us -> 0 us
  Pallas kernels: 0 us -> 263 us
  local copies, waits for them, and re-layouts: 134 us -> 64.9 us
  blocking collectives: 55.3 us -> 0 us
  matrix products: 169 us -> 140 us
  between operations: 17 us -> 4.16 us
    pallas_call x0 -> x2, Pallas kernels: none -> 263 us  [the longest x1 158 us: reduce_call(): pl.pallas_call(functools.partial(reduce_kernel, plan, wide), out_shape=ja...]
    all_gather x8 -> x0, waiting for transfers between devices: 248 us -> none  [the longest x4 183 us: gather_full(): return lax.all_gather(column, 'rep', axis=0, tiled=False)]
    unnamed x22 -> x0, waiting for transfers between devices: 195 us -> none
    all_gather x4 -> x0, blocking collectives: 55.3 us -> none  [the longest x3 35.9 us: reduce_full(): pieces = lax.all_gather(part, 'rep', axis=0, tiled=False)]
    reduce_scatter x2 -> x0, waiting for transfers between devices: 50.8 us -> none  [reduce_full(): part = lax.psum_scatter(part, 'shard', scatter_dimension=0, tiled=True)]
    unnamed x108 -> x170, local copies, waits for them, and re-layouts: 59.1 us -> 12.5 us
    dot_general x12 -> x8, matrix products: 84.2 us -> 60.3 us  [the longest x1 16.6 us: shards_fast(): jnp.dot(second_input, gate_up_full, preferred_element_type=jnp.float32)]
    dot_general x3 -> x1, local copies, waits for them, and re-layouts: 21.3 us -> 8.73 us  [shards_fast(): jnp.dot(first_input, in_full, preferred_element_type=jnp.float32)]
  transfers between devices with their start and end apart: 16 -> 0, of which waited for: 15 -> 0; matrix products, arithmetic and copies ran while one was open for 31% -> 0% of each run, Pallas kernels for 0% -> 0%
where the time goes in v2:
time: 543 us; the launch traced here: 539 us
  Pallas kernels  263 us (48%)
  matrix products  140 us (26%)
  other arithmetic  66.3 us (12%)
  local copies, waits for them, and re-layouts  64.9 us (12%)
    pallas_call x1, Pallas kernels, reduce_call(): pl.pallas_call(functools.partial(reduce_kernel, plan, wide), out_shape=ja...  158 us
    pallas_call x1, Pallas kernels, gather_call(): pl.pallas_call(functools.partial(gather_kernel, shapes, chunks, lags), ou...  106 us
    dot_general x1, matrix products, attend_backward(): jnp.einsum('hqk,qhd->khd', score_grad, queries, preferred_element_type=jn...  24.2 us
    sub x4, other arithmetic, adam_update(): weight - learn_rate[0] * (first_hat / (jnp.sqrt(second_hat) + adam_eps) +...  23.3 us
    dot_general x1, matrix products, attend_backward(): jnp.einsum('hqk,khd->qhd', score_grad, rotated_keys, preferred_element_ty...  23 us
    dot_general x1, matrix products, shards_fast(): jnp.dot(second_input, gate_up_full, preferred_element_type=jnp.float32)  16.6 us
    dot_general x1, matrix products, shards_fast(): jnp.einsum('rf,df->rd', gate_up_grad_low, gate_up_full, preferred_element...  12.9 us
    unnamed x170, local copies, waits for them, and re-layouts  12.5 us

profile of v2, /device:TPU:0, one launch (start us, length us, event | category | flops | bytes accessed | tf_op | source)
XLA Modules:
  0.0 538.5 jit_solution(16079771089192737489)
XLA Ops:
  21.4 105.5 %shard_map.313 = (bf16[1024,3072]{1,0:T(8,128)(2,1)}, bf16[1024,1024]{1,0:T(8,128)(2,1)}, bf16[1024,5632]{1,0:T(8,128)(2,1)}, bf16[2816,1024]{1,0:T(8,128)(2,1)}) custom-call(bf16[128,3072]{1,0:T(8,128)(2,1)} %copy.90.refs_0_, bf16[128,1024]{1,0:T(8,128)(2,1)} %convert_element_type.123.refs_1_, bf16[128,5632]{1,0:T(8,128)(2,1)} %bitcast.468, ...), custom_call_target="tpu_custom_call" | custom-call | tf_op jit(solution)/shard_map/pallas_call | solution.py:244
  127.0 8.7 %copy.91 = bf16[3072,1024]{1,0:T(8,128)(2,1)} copy(bf16[3072,1024]{0,1:T(8,128)(2,1)} %bitcast.464) | data formatting | bytes 12582912 | tf_op jit(solution)/shard_map/dot_general | solution.py:751
  135.7 5.8 %fusion.58 = f32[512,3,1024]{2,0,1:T(8,128)S(1)} fusion(bf16[3,1024,1024]{2,1,0:T(8,128)(2,1)} %bitcast.467, bf16[1,512,1024]{2,1,0:T(8,128)(2,1)S(1)} %copy-done.1, f32[512]{0:T(512)S(1)} %add_rsqrt_fusion.1, f32[512]{0:T(512)S(1)} %broadcast_multiply_fusion.5), kind=kOutput, calls=%fused_computation.88 | convolution fusion | flops 3223322624 | bytes 13635584 | tf_op jit(solution)/shard_map/dot_general | solution.py:751
  155.6 7.4 %fusion.94 = (f32[16,512]{1,0:T(8,128)S(1)}, f32[16,512,512]{1,2,0:T(8,128)}) fusion(bf16[512,16,64]{0,2,1:T(8,128)(2,1)S(1)} %get-tuple-element.143, bf16[512,16,64]{0,2,1:T(8,128)(2,1)S(1)} %get-tuple-element.142, pred[512,512]{0,1:T(8,128)(4,1)S(1)} %fusion.67), kind=kOutput, calls=%fused_computation.302 | convolution fusion | flops 549445632 | bytes 19169280 | tf_op jit(solution)/shard_map/while/body/eval_jaxpr/qhd,khd->hqk/dot_general | solution.py:54
  163.0 8.4 %fusion.4 = f32[16,512]{1,0:T(8,128)S(1)} fusion(f32[16,512,512]{1,2,0:T(8,128)} %get-tuple-element.148, f32[16,512]{1,0:T(8,128)S(1)} %get-tuple-element.147), kind=kLoop, calls=%fused_computation.8 | loop fusion | flops 8380416 | bytes 16842752 | tf_op jit(solution)/shard_map/while/body/eval_jaxpr/reduce_sum | solution.py:67
  171.4 7.5 %fusion.51 = bf16[16,64,512]{2,1,0:T(8,128)(2,1)S(1)} fusion(bf16[512,16,64]{0,2,1:T(8,128)(2,1)S(1)} %bitcast.470, f32[16,512,512]{1,2,0:T(8,128)} %get-tuple-element.148, f32[16,512]{1,0:T(8,128)S(1)} %fusion.4, f32[16,512]{1,0:T(8,128)S(1)} %get-tuple-element.147), kind=kOutput, calls=%fused_computation.79 | convolution fusion | flops 549978112 | bytes 18939904 | tf_op jit(solution)/shard_map/while/body/eval_jaxpr/hqk,khd->qhd/dot_general | solution.py:69
  184.6 16.6 %fusion.80 = f32[512,5632]{0,1:T(8,128)} fusion(bf16[1024,5632]{1,0:T(8,128)(2,1)} %get-tuple-element.75, f32[512,1024]{1,0:T(8,128)S(1)} %get-tuple-element.150, f32[512]{0:T(512)S(1)} %add_rsqrt_fusion, f32[512]{0:T(512)S(1)} %broadcast_multiply_fusion.4), kind=kOutput, calls=%fused_computation.294 | convolution fusion | flops 5907152896 | bytes 25169920 | tf_op jit(solution)/shard_map/dot_general | solution.py:766
  201.2 10.1 %multiply_convert_fusion.2 = (bf16[512,2816]{0,1:T(8,128)(2,1)}, bf16[512,2816]{0,1:T(8,128)(2,1)}, bf16[512,2816]{0,1:T(8,128)(2,1)S(1)}) fusion(f32[512,5632]{0,1:T(8,128)} %fusion.80, bf16[512,1024]{1,0:T(8,128)(2,1)S(1)} %copy-done.10, bf16[2816,1024]{1,0:T(8,128)(2,1)S(1)} %bitcast.497), kind=kOutput, calls=%fused_computation.18 | convolution fusion | flops 2975858688 | bytes 27000832 | tf_op jit(solution)/shard_map/re,fe->rf/dot_general | solution.py:776
  211.3 4.2 fusion.56
  215.5 12.9 %fusion.84 = (f32[512]{0:T(512)S(1)}, f32[512]{0:T(512)S(1)}, f32[512,1024]{1,0:T(8,128)}) fusion(f32[512]{0:T(512)S(1)} %add_rsqrt_fusion, f32[512,1024]{1,0:T(8,128)S(1)} %get-tuple-element.150, f32[512]{0:T(512)S(1)} %broadcast_multiply_fusion.4, bf16[1024,5632]{1,0:T(8,128)(2,1)} %get-tuple-element.75, bf16[512,2816]{0,1:T(8,128)(2,1)} %get-tuple-element.99, ...), kind=kOutput, calls=%fused_computation.297 | convolution fusion | flops 5919734784 | bytes 21504000 | tf_op jit(solution)/shard_map/rf,df->rd/dot_general | solution.py:782
  228.4 5.5 %pad_maximum_fusion = bf16[512,5632]{0,1:T(8,128)(2,1)} fusion(bf16[512,2816]{0,1:T(8,128)(2,1)} %get-tuple-element.99, bf16[512,2816]{0,1:T(8,128)(2,1)} %get-tuple-element.98), kind=kLoop, calls=%fused_computation.16 | loop fusion | flops 11534336 | bytes 11534336 | tf_op jit(solution)/shard_map/concatenate | solution.py:781
  233.9 8.3 %copy.112.refs_3_ = bf16[512,5632]{1,0:T(8,128)(2,1)} copy(bf16[512,5632]{0,1:T(8,128)(2,1)} %pad_maximum_fusion) | data formatting | bytes 11534336 | tf_op jit(solution)/shard_map/concatenate | solution.py:781
  242.3 3.6 fusion.89
  252.0 9.5 %fusion.52 = bf16[16,64,512]{2,1,0:T(8,128)(2,1)} fusion(bf16[512,16,64]{0,2,1:T(8,128)(2,1)S(1)} %bitcast.460, f32[16,512,512]{1,2,0:T(8,128)} %get-tuple-element.148, f32[16,512]{1,0:T(8,128)S(1)} %log_add_fusion), kind=kOutput, calls=%fused_computation.81 | convolution fusion | flops 545783808 | bytes 18907136 | tf_op jit(solution)/shard_map/while/body/eval_jaxpr/hqk,qhd->khd/dot_general | solution.py:80
  263.7 8.1 %fusion.96 = f32[16,512,512]{1,2,0:T(8,128)} fusion(bf16[512,16,64]{0,2,1:T(8,128)(2,1)S(1)} %bitcast.461, bf16[512,16,64]{0,2,1:T(8,128)(2,1)S(1)} %bitcast.471), kind=kOutput, calls=%fused_computation.304 | convolution fusion | flops 536870912 | bytes 18874368 | tf_op jit(solution)/shard_map/while/body/eval_jaxpr/qhd,khd->hqk/dot_general | solution.py:86
  271.9 23.0 %fusion.15 = f32[16,64,512]{2,1,0:T(8,128)S(1)} fusion(bf16[512,16,64]{0,2,1:T(8,128)(2,1)} %copy-done.18, f32[16,512,512]{1,2,0:T(8,128)} %fusion.96, f32[16,512,512]{1,2,0:T(8,128)} %get-tuple-element.148, f32[16,512]{1,0:T(8,128)S(1)} %log_add_fusion), kind=kOutput, calls=%fused_computation.15 | convolution fusion | flops 566239744 | bytes 36732928 | tf_op jit(solution)/shard_map/while/body/eval_jaxpr/hqk,khd->qhd/dot_general | solution.py:93
  294.8 24.2 %fusion.12 = f32[16,64,512]{2,1,0:T(8,128)} fusion(bf16[512,16,64]{0,2,1:T(8,128)(2,1)} %copy-done.17, f32[16,512,512]{1,2,0:T(8,128)} %fusion.96, f32[16,512,512]{1,2,0:T(8,128)} %get-tuple-element.148, f32[16,512]{1,0:T(8,128)S(1)} %log_add_fusion), kind=kOutput, calls=%fused_computation.14 | convolution fusion | flops 566239744 | bytes 36732928 | tf_op jit(solution)/shard_map/while/body/eval_jaxpr/hqk,qhd->khd/dot_general | solution.py:96
  323.4 5.1 fusion.83
  341.9 157.6 %shard_map.314 = bf16[10,4,2,16,1408]{4,3,2,1,0:T(8,128)(2,1)} custom-call(bf16[2048,512]{1,0:T(8,128)(2,1)} %copy.110.refs_0_, bf16[512,4096]{1,0:T(8,128)(2,1)} %pad_maximum_fusion.1.refs_1_, bf16[1024,512]{1,0:T(8,128)(2,1)} %copy.111.refs_2_, bf16[512,5632]{1,0:T(8,128)(2,1)} %copy.112.refs_3_, bf16[2816,512]{1,0:T(8,128)(2,1)} %bitcast.482, ...), custom_call_target="tpu_custom_call" | custom-call | tf_op jit(solution)/shard_map/pallas_call | solution.py:477
  508.8 3.8 reshape.401
  512.7 3.8 multiply_subtract_fusion.3
  516.6 4.5 multiply_subtract_fusion.2
  521.2 3.6 multiply_subtract_fusion.1
  527.0 11.4 %multiply_subtract_fusion = (f32[128,2,2816]{2,1,0:T(2,128)}, f32[128,2,2816]{2,1,0:T(2,128)}, f32[128,2,2816]{2,1,0:T(2,128)}) fusion(f32[128,2,2816]{2,1,0:T(2,128)S(1)} %copy-done.3, f32[]{:T(128)} %bitcast.74, f32[]{:T(128)} %bitcast.73, f32[]{:T(128)} %bitcast.454, f32[128,2,2816]{2,1,0:T(2,128)S(1)} %reshape.401, f32[128,2,2816]{2,1,0:T(2,128)S(1)} %copy-done.24, ...), kind=kLoop, calls=%fused_computation.33 | loop fusion | flops 10813440 | bytes 20185100 | tf_op jit(solution)/shard_map/sub | solution.py:106
  (250 shorter events, 75.2 us)
Async XLA Ops:
  0.7 10.1 %copy-start.8 = (f32[352,1024]{1,0:T(8,128)S(1)}, f32[352,1024]{1,0:T(8,128)}, u32[]{:S(2)}) copy-start(f32[352,1024]{1,0:T(8,128)} %param.33) | copy-start | bytes 4325380
  11.8 7.4 %copy-start.2 = (f32[128,2,2816]{2,1,0:T(2,128)S(1)}, f32[128,2,2816]{2,1,0:T(2,128)}, u32[]{:S(2)}) copy-start(f32[128,2,2816]{2,1,0:T(2,128)} %param.30) | copy-start | bytes 8650756
  127.0 8.7 %copy-start.1 = (bf16[1,512,1024]{2,1,0:T(8,128)(2,1)S(1)}, bf16[1,512,1024]{2,1,0:T(8,128)(2,1)}, u32[]{:S(2)}) copy-start(bf16[1,512,1024]{2,1,0:T(8,128)(2,1)} %param.18) | copy-start | bytes 3145732
  155.5 7.5 %copy-start.17 = (bf16[512,16,64]{0,2,1:T(8,128)(2,1)}, bf16[512,16,64]{0,2,1:T(8,128)(2,1)S(1)}, u32[]{:S(2)}) copy-start(bf16[512,16,64]{0,2,1:T(8,128)(2,1)S(1)} %get-tuple-element.143) | copy-start | bytes 3145732
  155.5 7.5 %copy-start.18 = (bf16[512,16,64]{0,2,1:T(8,128)(2,1)}, bf16[512,16,64]{0,2,1:T(8,128)(2,1)S(1)}, u32[]{:S(2)}) copy-start(bf16[512,16,64]{0,2,1:T(8,128)(2,1)S(1)} %get-tuple-element.142) | copy-start | bytes 3145732
  163.0 8.4 %copy-start.11 = (bf16[512,1,1024]{0,2,1:T(8,128)(2,1)S(1)}, bf16[512,1,1024]{0,2,1:T(8,128)(2,1)}, u32[]{:S(2)}) copy-start(bf16[512,1,1024]{0,2,1:T(8,128)(2,1)} %copy.92) | copy-start | bytes 3145732
  180.8 20.4 %slice-start.2 = ((s8[5767168]{0:T(1024)(128)(4,1)}), s8[4194304]{0:T(1024)(128)(4,1)S(1)}, s32[]{:S(2)}) async-start(s8[5767168]{0:T(1024)(128)(4,1)} %bitcast.496), calls=%async_computation.2 | async-start | bytes 8388608
  184.6 16.6 %copy-start.10 = (bf16[512,1024]{1,0:T(8,128)(2,1)S(1)}, bf16[512,1024]{1,0:T(8,128)(2,1)}, u32[]{:S(2)}) copy-start(bf16[512,1024]{1,0:T(8,128)(2,1)} %fusion.48.refs_5_) | copy-start | bytes 3145732
  184.6 16.6 %slice-start.3 = ((s8[5767168]{0:T(1024)(128)(4,1)}), s8[1572864]{0:T(1024)(128)(4,1)S(1)}, s32[]{:S(2)}) async-start(s8[5767168]{0:T(1024)(128)(4,1)} %bitcast.496), calls=%async_computation.3 | async-start | bytes 3145728
  211.3 4.2 copy-start.26
  242.3 4.6 copy-start.29
  252.0 11.8 %copy-start.12 = (bf16[512,1,1024]{0,2,1:T(8,128)(2,1)S(1)}, bf16[512,1,1024]{0,2,1:T(8,128)(2,1)}, u32[]{:S(2)}) copy-start(bf16[512,1,1024]{0,2,1:T(8,128)(2,1)} %copy.92) | copy-start | bytes 3145732
  319.0 4.4 slice-start
  328.5 4.7 copy-start.20
  328.5 4.7 copy-start.21
  512.7 12.1 %copy-start.4 = (f32[128,2,2816]{2,1,0:T(2,128)}, f32[128,2,2816]{2,1,0:T(2,128)S(1)}, u32[]{:S(2)}) copy-start(f32[128,2,2816]{2,1,0:T(2,128)S(1)} %reshape.401) | copy-start | bytes 8650756
  516.5 4.6 copy-start.7
  516.6 4.6 copy-start.30
  516.6 4.6 copy-start.31
  516.6 4.6 copy-start.39
  516.6 4.6 copy-start.41
  516.6 4.6 copy-start.43
  521.2 4.9 copy-start.24
  521.2 5.7 %copy-start.25 = (f32[128,2,2816]{2,1,0:T(2,128)S(1)}, f32[128,2,2816]{2,1,0:T(2,128)}, u32[]{:S(2)}) copy-start(f32[128,2,2816]{2,1,0:T(2,128)} %param.31) | copy-start | bytes 8650756
  (24 other events, 56.8 us)

commit v3 on v1

--- a/solution.py
+++ b/solution.py
@@ -1,7 +1,16 @@
+import functools
+
 import jax
 import jax.numpy as jnp
 from jax import lax
+from jax.experimental import pallas as pl
+from jax.experimental.pallas import tpu as pltpu
 from jax.sharding import PartitionSpec as P
+
+MESH = pl.DeviceIdType.MESH
+DMA = pltpu.SemaphoreType.DMA
+RING = 4
+F32, BF16 = jnp.float32, jnp.bfloat16
 
 HD = 64
 
@@ -101,6 +110,752 @@
     return (gradient, weight_new, first_new, second_new)
 
 
+class Gather:
+    @staticmethod
+    def scratch(tensors, chunks):
+        return [DMA((tensors,)), DMA((chunks, 4)), DMA((chunks, 4)), DMA((chunks, 2, 3)), DMA((chunks, 2, 3))] + [DMA((chunks, 3, 2))] * 4
+
+    def __init__(self, shapes, chunks, loc, full, sems):
+        self.shapes, self.chunks, self.loc, self.full = shapes, chunks, loc, full
+        (self.own_s, self.sib_s, self.sib_r, self.z_s, self.z_r, self.p_s, self.p_r, self.d_s, self.d_r) = sems
+        self.rep, self.shard = lax.axis_index("rep"), lax.axis_index("shard")
+        self.z, core = self.shard // 2, lax.rem(self.shard, 2)
+        x, y = lax.rem(self.rep, 2), self.rep // 2
+        self.sib = (self.rep, self.shard + 1 - 2 * core)
+        self.nb = ((self.rep + 1 - 2 * x, self.shard), (self.rep + 2 - 4 * y, self.shard))
+        self.diag = self.rep + (1 - 2 * x) + (2 - 4 * y)
+
+    def barrier(self):
+        bar = pltpu.get_barrier_semaphore()
+        for dev in (self.sib,) + self.nb + tuple((self.rep, self.other(d)) for d in (1, 2, 3)):
+            pl.semaphore_signal(bar, inc=1, device_id=dev, device_id_type=MESH)
+        pl.semaphore_wait(bar, 6)
+
+    def ref(self, c, s, q=None, half=None):
+        t, r0, rows, c0, cols, axis = self.chunks[c]
+        base, col, nr, nc = s * self.shapes[t][0] + r0, c0, rows, cols
+        if q is not None:
+            parts, i = (4, q) if half is None else (8, 2 * q + half)
+            if axis == 0:
+                nr = rows // parts
+                base = base + i * nr
+            else:
+                nc = cols // parts
+                col = pl.multiple_of(c0 + i * nc, 128)
+        return self.full[t].at[pl.ds(pl.multiple_of(base, 16), nr), pl.ds(col, nc)]
+
+    def loc_ref(self, c, q=None):
+        t, r0, rows, c0, cols, axis = self.chunks[c]
+        row, col, nr, nc = r0, c0, rows, cols
+        if q is not None and axis == 0:
+            nr = rows // 4
+            row = pl.multiple_of(r0 + q * nr, 16)
+        elif q is not None:
+            nc = cols // 4
+            col = pl.multiple_of(c0 + q * nc, 128)
+        return self.loc[t].at[pl.ds(row, nr), pl.ds(col, nc)]
+
+    def copy(self, src, dst, s, r, dev):
+        return pltpu.make_async_remote_copy(src_ref=src, dst_ref=dst, send_sem=s, recv_sem=r, device_id=dev, device_id_type=MESH)
+
+    def own(self, t):
+        rows = self.shapes[t][0]
+        return pltpu.make_async_copy(self.loc[t], self.full[t].at[pl.ds(pl.multiple_of(self.shard * rows, rows), rows), :], self.own_s.at[t])
+
+    def other(self, dz):
+        return lax.rem(self.shard + 2 * dz, 8)
+
+    def sibling(self, c, dz):
+        r = self.ref(c, self.other(dz))
+        return self.copy(self.loc_ref(c) if dz == 0 else r, r, self.sib_s.at[c, dz], self.sib_r.at[c, dz], self.sib)
+
+    def chain(self, c, side, h):
+        sgn = 1 if side == 0 else -1
+        s = self.shard - sgn * 2 * (h - 1)
+        src = self.loc_ref(c, self.rep) if h == 1 else self.ref(c, s, self.rep)
+        return self.copy(src, self.ref(c, s, self.rep), self.z_s.at[c, side, h - 1], self.z_r.at[c, side, h - 1], (self.rep, self.shard + sgn * 2))
+
+    def chain_in(self, c, side, h):
+        sgn = 1 if side == 0 else -1
+        r = self.ref(c, self.shard - sgn * 2 * h, self.rep)
+        return self.copy(r, r, self.z_s.at[c, side, h - 1], self.z_r.at[c, side, h - 1], (self.rep, self.shard - sgn * 2))
+
+    def chain_sends(self, side, h):
+        if side == 0:
+            return jnp.logical_and(self.z < 3, self.z >= h - 1)
+        return jnp.logical_and(self.z > 0, self.z <= 4 - h)
+
+    def plane(self, c, dz, k, theirs=False):
+        r = self.ref(c, self.other(dz), self.nb[k][0] if theirs else self.rep)
+        return self.copy(r, r, self.p_s.at[c, dz - 1, k], self.p_r.at[c, dz - 1, k], self.nb[k])
+
+    def corner(self, c, dz, k, theirs=False):
+        r = self.ref(c, self.other(dz), self.diag if theirs else self.nb[k][0], k)
+        return self.copy(r, r, self.d_s.at[c, dz - 1, k], self.d_r.at[c, dz - 1, k], self.nb[1 - k])
+
+    def s0(self, c):
+        for side in (0, 1):
+            @pl.when(self.chain_sends(side, 1))
+            def _():
+                self.chain(c, side, 1).start()
+        self.sibling(c, 0).start()
+
+    def s1(self, c, h):
+        for side in (0, 1):
+            @pl.when((self.z >= h) if side == 0 else (self.z <= 3 - h))
+            def _():
+                self.chain_in(c, side, h).wait_recv()
+                if h < 3:
+                    @pl.when((self.z < 3) if side == 0 else (self.z > 0))
+                    def _():
+                        self.chain(c, side, h + 1).start()
+                for k in (0, 1):
+                    self.plane(c, (4 - h) if side == 0 else h, k).start()
+
+    def s2(self, c):
+        for dz in (1, 3, 2):
+            for k in (0, 1):
+                self.plane(c, dz, k, True).wait_recv()
+                self.corner(c, dz, k).start()
+
+    def s3(self, c):
+        for dz in (1, 3, 2):
+            for k in (0, 1):
+                self.corner(c, dz, k, True).wait_recv()
+            self.sibling(c, dz).start()
+
+    def s4(self, c):
+        for dz in range(4):
+            self.sibling(c, dz).wait()
+
+    def drain(self, c):
+        for side in (0, 1):
+            for h in (1, 2, 3):
+                @pl.when(self.chain_sends(side, h))
+                def _():
+                    self.chain(c, side, h).wait_send()
+        for dz in (1, 2, 3):
+            for k in (0, 1):
+                self.plane(c, dz, k).wait_send()
+                self.corner(c, dz, k).wait_send()
+
+
+def normed(v):
+    c = v - jnp.mean(v, axis=-1, keepdims=True)
+    inv = lax.rsqrt(jnp.mean(c * c, axis=-1, keepdims=True) + norm_eps)
+    return c * inv, inv
+
+
+def turn(w):
+    lane = lax.broadcasted_iota(jnp.int32, w.shape, 1)
+    return jnp.where(lax.rem(lane, 64) < 32, pltpu.roll(w, 96, 1), pltpu.roll(w, 32, 1))
+
+
+def two_heads(w):
+    lane = lax.broadcasted_iota(jnp.int32, w.shape, 1)
+    zero = jnp.zeros_like(w)
+    return jnp.concatenate([jnp.where(lane < 64, w, zero), jnp.where(lane < 64, zero, w)], axis=0)
+
+
+def join_heads(w):
+    n = w.shape[0] // 2
+    lane = lax.broadcasted_iota(jnp.int32, (n, w.shape[1]), 1)
+    return jnp.where(lane < 64, w[:n], w[n:])
+
+
+def dot(a, b, da=1, db=0):
+    return lax.dot_general(a, b, (((da,), (db,)), ((), ())), preferred_element_type=F32)
+
+
+def probabilities(q2, keys, bias):
+    n, width = q2.shape[0] // 2, keys.shape[0]
+    s = dot(q2, keys, 1, 1) * 0.125 + bias
+    row = lax.broadcasted_iota(jnp.int32, (n, 128), 0)
+    col = lax.broadcasted_iota(jnp.int32, (n, 128), 1)
+    causal = jnp.where(col <= row, 0.0, -1e30)
+    last = s[:, width - 128:] + jnp.concatenate([causal, causal], axis=0)
+    s = last if width == 128 else jnp.concatenate([s[:, :width - 128], last], axis=1)
+    e = jnp.exp(s - jnp.max(s, axis=-1, keepdims=True))
+    return e * (1.0 / jnp.sum(e, axis=-1, keepdims=True))
+
+
+def forward_kernel(
+    shapes, chunks,
+    x_ref, bias_ref, cos_ref, sin_ref, win_h, wout_h, wgu_h, wdn_h,
+    fin_h, fout_h, fgu_h, fdn_h, at_h, ot_h, bt_h, mt_h, qkv_h, slopes_h, h_h,
+    win, wout, wgu, wdn, lin, lout, lgu, ldn, bin_, bout, bgu,
+    a, at, qkv, o, ot, h, b, bt, mt, slopes, in_s, load_s, out_s, *sems,
+):
+    g = Gather(shapes, chunks, (lin, lout, lgu, ldn), (fin_h, fout_h, fgu_h, fdn_h), sems)
+    rows = x_ref.shape[0]
+    loads = [pltpu.make_async_copy(s, d, in_s.at[i]) for i, (s, d) in enumerate(((win_h, win), (wout_h, wout), (wgu_h, wgu), (wdn_h, wdn)))]
+    for cp in loads:
+        cp.start()
+    outs = [pltpu.make_async_copy(s, d, out_s.at[i]) for i, (s, d) in enumerate(
+        ((at, at_h), (ot, ot_h), (bt, bt_h), (mt, mt_h), (qkv, qkv_h), (slopes, slopes_h), (h, h_h)))]
+    AT, OT, BT, MT, QKV, SL, H = range(7)
+    g.barrier()
+
+    def weight_in(t):
+        loads[t].wait()
+        if t == 0:
+            for p in range(3):
+                lin[:, 1024 * p:1024 * p + 1024] = win[p].astype(BF16)
+        elif t == 1:
+            lout[...] = wout[...].astype(BF16)
+        elif t == 3:
+            ldn[...] = wdn[...].astype(BF16)
+        else:
+            tiles = lgu.shape[1] // 128
+            for c in range(tiles):
+                lgu[:, 128 * c:128 * c + 128] = wgu[pl.ds(c, lgu.shape[0], stride=tiles), :].astype(BF16)
+        g.own(t).start()
+
+    def ln_one():
+        for r in range(0, rows, 128):
+            n, _ = normed(x_ref[r:r + 128, :].astype(F32))
+            a[r:r + 128, :] = n.astype(BF16)
+        for c in range(0, 1024, 128):
+            at[c:c + 128, :] = a[:, c:c + 128].T
+        outs[AT].start()
+
+    def load(t, c0, n, dst):
+        return pltpu.make_async_copy(g.full[t].at[:, pl.ds(c0, n)], dst.at[:, pl.ds(c0, n)], load_s.at[t])
+
+    def project(p, j):
+        c = 1024 * p + 256 * j
+        w = dot(a[...], bin_[:, c:c + 256])
+        for i in (0, 128):
+            t = w[:, i:i + 128]
+            if p < 2:
+                t = t * cos_ref[...] + turn(t) * sin_ref[...]
+            qkv[:, c + i:c + i + 128] = t.astype(BF16)
+
+    def attend(pair):
+        for qt in range(rows // 128):
+            width = 128 * (qt + 1)
+            lo = pl.multiple_of(pair * 128, 128)
+            q2 = two_heads(qkv[128 * qt:width, pl.ds(lo, 128)])
+            p = probabilities(q2, qkv[:width, pl.ds(pl.multiple_of(1024 + lo, 128), 128)], bias_ref[:, :width])
+            mixed = join_heads(dot(p.astype(BF16), qkv[:width, pl.ds(pl.multiple_of(2048 + lo, 128), 128)]))
+            o[128 * qt:width, pl.ds(lo, 128)] = mixed.astype(BF16)
+        ot[pl.ds(lo, 128), :] = o[:, pl.ds(lo, 128)].T
+
+    def out_and_norm():
+        for r in range(0, rows, 256):
+            v = x_ref[r:r + 256, :].astype(F32) + dot(o[r:r + 256, :], bout[...])
+            h[r:r + 256, :] = v
+            n, _ = normed(v)
+            b[r:r + 256, :] = n.astype(BF16)
+        outs[H].start()
+        for c in range(0, 1024, 128):
+            bt[c:c + 128, :] = b[:, c:c + 128].T
+        outs[BT].start()
+
+    def gate(ct):
+        lo = pl.multiple_of(ct * 256, 256)
+        w = dot(b[...], bgu[:, pl.ds(lo, 256)])
+        gv, uv = w[:, :128], w[:, 128:]
+        sig = jax.nn.sigmoid(gv)
+        silu = gv * sig
+        mt[pl.ds(pl.multiple_of(ct * 128, 128), 128), :] = (silu * uv).astype(BF16).T
+        slopes[:, pl.ds(lo, 128)] = (uv * sig * (1.0 + gv * (1.0 - sig))).astype(BF16)
+        slopes[:, pl.ds(pl.multiple_of(lo + 128, 128), 128)] = silu.astype(BF16)
+
+    Q, O, G1, G2, D = range(5)
+    half = chunks[G1][4]
+    tiles = half // 256
+    weight_in(0)
+    g.s0(Q)
+    weight_in(1)
+    g.s0(O)
+    ln_one()
+    g.s1(Q, 1)
+    weight_in(2)
+    g.s1(Q, 2)
+    g.s0(G1)
+    g.s1(O, 1)
+    g.s1(O, 2)
+    g.s1(Q, 3)
+    g.s2(Q)
+    g.s0(G2)
+    weight_in(3)
+    g.s1(G1, 1)
+    g.s1(G1, 2)
+    g.s1(O, 3)
+    g.s2(O)
+    g.s3(Q)
+    g.s0(D)
+    g.s1(G2, 1)
+    g.s4(Q)
+    g.own(0).wait()
+    ld = load(0, 0, chunks[Q][4], bin_)
+    ld.start()
+    g.s1(G2, 2)
+    g.s1(G1, 3)
+    ld.wait()
+    between = {
+        (0, 1): lambda: g.s2(G1), (1, 3): lambda: g.s3(O), (2, 3): lambda: g.s1(D, 1),
+    }
+    for p in range(3):
+        for j in range(4):
+            project(p, j)
+            if (p, j) in between:
+                between[p, j]()
+    outs[QKV].start()
+    steps = [lambda: g.s1(D, 2), lambda: g.s1(G2, 3), lambda: g.s2(G2), lambda: g.s3(G1)]
+    for i in range(4):
+        lax.fori_loop(2 * i, 2 * i + 2, lambda k, _: (attend(k), 0)[1], 0)
+        steps[i]()
+        if i == 1:
+            g.s4(O)
+            g.own(1).wait()
+            ld = load(1, 0, 1024, bout)
+            ld.start()
+    outs[OT].start()
+    ld.wait()
+    out_and_norm()
+    g.s1(D, 3)
+    g.s2(D)
+    g.own(2).wait()
+    g.s4(G1)
+    ld = load(2, 0, half, bgu)
+    ld.start()
+    g.s3(G2)
+    ld.wait()
+    mid = tiles // 2
+    lax.fori_loop(0, mid, lambda k, _: (gate(k), 0)[1], 0)
+    g.s4(G2)
+    ld = load(2, half, half, bgu)
+    ld.start()
+    lax.fori_loop(mid, tiles, lambda k, _: (gate(k), 0)[1], 0)
+    g.s3(D)
+    ld.wait()
+    lax.fori_loop(tiles, 2 * tiles, lambda k, _: (gate(k), 0)[1], 0)
+    outs[MT].start()
+    outs[SL].start()
+    g.s4(D)
+    g.own(3).wait()
+    for c in range(len(chunks)):
+        g.drain(c)
+    for cp in outs:
+        cp.wait()
+
+
+def forward_call(x, bias, cos, sin, win, wout, wgu, wdn):
+    rows, d = x.shape
+    r = wout.shape[0]
+    ff2 = wgu.shape[0] * 128 // r
+    ff = ff2 // 2
+    shapes = ((r, 3 * d), (r, d), (r, ff2), wdn.shape)
+    chunks = ((0, 0, r, 0, 3 * d, 1), (1, 0, r, 0, d, 1), (2, 0, r, 0, ff, 0), (2, 0, r, ff, ff, 0), (3, 0, wdn.shape[0], 0, d, 1))
+    vm, an = pl.BlockSpec(memory_space=pltpu.VMEM), pl.BlockSpec(memory_space=pl.ANY)
+    sd = lambda s, t=BF16: jax.ShapeDtypeStruct(s, t)
+    v = lambda s, t=BF16: pltpu.VMEM(s, t)
+    outs = [sd((8 * s[0], s[1])) for s in shapes] + [sd((d, rows)), sd((d, rows)), sd((d, rows)), sd((ff, rows)), sd((rows, 3 * d)), sd((rows, ff2)), sd((rows, d), F32)]
+    scratch = [v(win.shape, F32), v(wout.shape, F32), v(wgu.shape, F32), v(wdn.shape, F32)] + [v(s) for s in shapes]
+    scratch += [v((8 * r, 3 * d)), v((8 * r, d)), v((8 * r, ff2))]
+    scratch += [v((rows, d)), v((d, rows)), v((rows, 3 * d)), v((rows, d)), v((d, rows)), v((rows, d), F32), v((rows, d)), v((d, rows)), v((ff, rows)), v((rows, ff2))]
+    scratch += [DMA((4,)), DMA((4,)), DMA((7,))] + Gather.scratch(4, len(chunks))
+    return pl.pallas_call(
+        functools.partial(forward_kernel, shapes, chunks),
+        out_shape=outs, in_specs=[vm] * 4 + [an] * 4, out_specs=[an] * len(outs), scratch_shapes=scratch,
+        compiler_params=pltpu.CompilerParams(collective_id=0, has_side_effects=True, vmem_limit_bytes=60 << 20),
+    )(x, bias, cos, sin, win, wout, wgu, wdn)
+
+
+class Reduce:
+    def __init__(self, refs):
+        (self.mine, self.theirs, self.held, self.sums, self.one, self.two, self.fin, self.planes, self.total,
+         self.a_s, self.a_r, self.o_s, self.o_r, self.t_s, self.t_r, self.c_s, self.c_r, self.d_s, self.d_r, self.f_s, self.f_r) = refs
+        self.rep, self.shard = lax.axis_index("rep"), lax.axis_index("shard")
+        self.core = lax.rem(self.shard, 2)
+        self.x, self.y = lax.rem(self.rep, 2), self.rep // 2
+        self.sib = (self.rep, self.shard + 1 - 2 * self.core)
+        self.nb = ((self.rep + 1 - 2 * self.x, self.shard), (self.rep + 2 - 4 * self.y, self.shard))
+
+    @staticmethod
+    def scratch(chunks, wide):
+        v = lambda *s: pltpu.VMEM(s, BF16)
+        return [
+            v(RING, 8, 16, wide),
+            v(RING, 8, 16, wide),
+            pltpu.VMEM((2, 8, 16, wide), F32),
+            v(RING, 8, 16, wide),
+            v(2, RING, 2, 16, wide),
+            v(2, RING, 16, wide),
+            v(RING, 2, 16, wide),
+            v(chunks, 3, 2, 16, wide),
+        ], [DMA((RING,)), DMA((RING,)), DMA((2, RING)), DMA((2, RING)), DMA((2, RING)), DMA((2, RING)), DMA((RING,)), DMA((chunks, 3)),
+            DMA((chunks, 2)), DMA((chunks, 2)), DMA((chunks, 2)), DMA((chunks, 2))]
+
+    def copy(self, src, dst, s, r, dev):
+        return pltpu.make_async_remote_copy(src_ref=src, dst_ref=dst, send_sem=s, recv_sem=r, device_id=dev, device_id_type=MESH)
+
+    def barrier(self):
+        bar = pltpu.get_barrier_semaphore()
+        for dev in (self.sib,) + self.nb + tuple((self.rep, lax.rem(self.shard + 2 * d, 8)) for d in (1, 2, 3)):
+            pl.semaphore_signal(bar, inc=1, device_id=dev, device_id_type=MESH)
+        pl.semaphore_wait(bar, 6)
+
+    def first(self, u, w):
+        s = lax.rem(u, RING)
+        return self.copy(self.mine.at[s, :, :, pl.ds(0, w)], self.theirs.at[s, :, :, pl.ds(0, w)], self.a_s.at[s], self.a_r.at[s], self.sib)
+
+    def hop_one(self, u, w, k):
+        s = lax.rem(u, RING)
+        at = 2 - 2 * self.x if k == 0 else 6 - 2 * self.y
+        return self.copy(self.sums.at[s, pl.ds(at, 2), :, pl.ds(0, w)], self.one.at[k, s, :, :, pl.ds(0, w)], self.o_s.at[k, s], self.o_r.at[k, s], self.nb[k])
+
+    def hop_two(self, u, w, k):
+        s = lax.rem(u, RING)
+        at = 2 * self.x + 1 - self.y if k == 0 else 4 + 2 * self.y + 1 - self.x
+        return self.copy(self.sums.at[s, at, :, pl.ds(0, w)], self.two.at[k, s, :, pl.ds(0, w)], self.t_s.at[k, s], self.t_r.at[k, s], self.nb[1 - k])
+
+    def across(self, u, w, dz):
+        s = lax.rem(u, RING)
+        c = u // 4
+        return self.copy(self.fin.at[s, :, :, pl.ds(0, w)], self.planes.at[c, 3 - dz, :, :, pl.ds(0, w)], self.c_s.at[s], self.c_r.at[c, 3 - dz], (self.rep, lax.rem(self.shard + 2 * dz, 8)))
+
+    def plane_in(self, c, w, j):
+        return self.copy(self.fin.at[0, :, :, pl.ds(0, w)], self.planes.at[c, j, :, :, pl.ds(0, w)], self.c_s.at[0], self.c_r.at[c, j], self.sib)
+
+    def spread(self, c, w, k, own=True):
+        q = self.rep if own else self.nb[k][0]
+        ref = self.total.at[c, q, :, :, pl.ds(0, w)]
+        return self.copy(ref, ref, self.d_s.at[c, k], self.d_r.at[c, k], self.nb[k])
+
+    def spread_on(self, c, w, k, own=True):
+        q = self.nb[k][0] if own else self.nb[0][0] + self.nb[1][0] - self.rep
+        ref = self.total.at[c, q, k, :, pl.ds(0, w)]
+        return self.copy(ref, ref, self.f_s.at[c, k], self.f_r.at[c, k], self.nb[1 - k])
+
+    def stage_two(self, u, w):
+        s = lax.rem(u, RING)
+        self.first(u, w).wait()
+        self.sums[s, :, :, :w] = (self.held[lax.rem(u, 2), :, :, :w] + self.theirs[s, :, :, :w].astype(F32)).astype(BF16)
+        for k in (0, 1):
+            self.hop_one(u, w, k).start()
+
+    def stage_three(self, u, w):
+        s = lax.rem(u, RING)
+        for k in (0, 1):
+            self.hop_one(u, w, k).wait()
+            at = 2 * self.x if k == 0 else 4 + 2 * self.y
+            new = self.sums[s, pl.ds(at, 2), :, :w].astype(F32) + self.one[k, s, :, :, :w].astype(F32)
+            self.sums[s, pl.ds(at, 2), :, :w] = new.astype(BF16)
+            self.hop_two(u, w, k).start()
+
+    def stage_four(self, u, w, start):
+        s = lax.rem(u, RING)
+        c = u // 4
+        dz = lax.rem(lax.rem(u, 4) + 1, 4)
+
+        @pl.when(jnp.logical_and(u >= start + RING, dz > 0))
+        def _():
+            self.across(u - RING, w, dz).wait_send()
+
+        for k in (0, 1):
+            self.hop_two(u, w, k).wait()
+
+        def plane_sum(k):
+            at = 2 * self.x + self.y if k == 0 else 4 + 2 * self.y + self.x
+            return self.sums[s, at, :, :w].astype(F32) + self.two[k, s, :, :w].astype(F32)
+
+        @pl.when(dz > 0)
+        def _():
+            for k in (0, 1):
+                self.fin[s, k, :, :w] = plane_sum(k).astype(BF16)
+            self.across(u, w, dz).start()
+
+        @pl.when(dz == 0)
+        def _():
+            for j in range(3):
+                self.plane_in(c, w, j).wait_recv()
+            for k in (0, 1):
+                out = plane_sum(k)
+                for j in range(3):
+                    out = out + self.planes[c, j, k, :, :w].astype(F32)
+                self.total[c, self.rep, k, :, :w] = out.astype(BF16)
+            for k in (0, 1):
+                self.spread(c, w, k).start()
+
+    def stage_five(self, u, w):
+        @pl.when(lax.rem(u, 4) == 3)
+        def _():
+            c = u // 4
+            for k in (0, 1):
+                self.spread(c, w, k, False).wait_recv()
+                self.spread_on(c, w, k).start()
+
+    def drain_across(self, units, w):
+        for u in range(units - RING, units):
+            if u % 4 != 3:
+                self.across(u, w, u % 4 + 1).wait_send()
+
+    def finish(self, units, width):
+        self.drain_across(units, width(units - 1))
+        for c in range(units // 4):
+            w = width(4 * c)
+            for k in (0, 1):
+                self.spread(c, w, k).wait_send()
+                self.spread_on(c, w, k).wait_send()
+                self.spread_on(c, w, k, False).wait_recv()
+
+
+def norm_back_rows(v, d):
+    n, inv = normed(v)
+    return inv * (d - jnp.mean(d, axis=-1, keepdims=True) - n * jnp.mean(d * n, axis=-1, keepdims=True))
+
+
+def backward_kernel(
+    wide,
+    x_ref, dy, live, bias_ref, cos_ref, sin_ref, at_h, ot_h, bt_h, mt_h, qkv_h, slopes_h, h_h, fin_h, fout_h, fgu_h, fdn_h,
+    total, out_h, grad_h,
+    atl, bt, mt, qkv, dgu, h, wd, wb, wo, atr, do, acc, dh, dk, dv, ld_s, wb_s, st_s, *rs,
+):
+    r = Reduce(rs[:8] + (total,) + rs[8:])
+    rows, d = x_ref.shape
+    chunk_plan = ((0, 2, wide), (1, 4, wide), (2, 4, d))
+    bounds, u0 = [], 0
+    for kind, n, w in chunk_plan:
+        bounds.append((u0, u0 + 4 * n, kind, w))
+        u0 += 4 * n
+    units = u0
+    names = ("mt", "wd", "gu", "bt", "qkv", "h", "wo", "ot", "at")
+    pairs = ((mt_h, mt), (fdn_h, wd), (slopes_h, dgu), (bt_h, bt), (qkv_h, qkv), (h_h, h), (fout_h, wo),
+             (ot_h, atl.at[pl.ds(d, d), :]), (at_h, atl.at[pl.ds(0, d), :]))
+    loads = {n: pltpu.make_async_copy(s, t, ld_s.at[i]) for i, (n, (s, t)) in enumerate(zip(names, pairs))}
+    for n in names:
+        loads[n].start()
+
+    def weights(j):
+        src = fgu_h.at[:, pl.ds(wide * j, wide)] if j < 4 else fin_h.at[:, pl.ds(d * (j - 4), d)]
+        dst = wb.at[j % 2] if j < 4 else wb.at[j % 2, :, pl.ds(0, d)]
+        return pltpu.make_async_copy(src, dst, wb_s.at[j % 2])
+
+    def width(u):
+        for a, b, _, w in bounds:
+            if a <= u < b:
+                return w
+
+    def start_of(w):
+        return min(a for a, _, _, v in bounds if v == w)
+
+    def product(u, kind, first, own):
+        c = u // 4 - first // 4
+        zt = lax.rem(r.shard // 2 + lax.rem(u, 4) + 1, 4)
+        core = r.core if own else 1 - r.core
+
+        def put(e, lo, n, val):
+            if own:
+                r.held[lax.rem(u, 2), e, :, lo:lo + n] = val
+            else:
+                r.mine[lax.rem(u, RING), e, :, lo:lo + n] = val.astype(BF16)
+
+        if kind == 0:
+            part = mt.shape[0] // 16
+            left = mt[pl.ds(pl.multiple_of((2 * zt + core) * 2 * part + c * part, 16), part), :]
+            for e in range(0, 8, 2):
+                val = dot(left, dy[:, e * 128:e * 128 + 256])
+                for i in (0, 1):
+                    for j in range(part // 16):
+                        put(e + i, 128 * j, 128, val[16 * j:16 * j + 16, i * 128:i * 128 + 128])
+            return
+        base = (2 * zt + core) * 128
+        if kind == 1:
+            left = bt[pl.ds(pl.multiple_of(base, 128), 128), :]
+            right, n = dgu[:, pl.ds(pl.multiple_of(c * wide, 128), wide)], wide
+        else:
+            left = atl[pl.ds(pl.multiple_of(base + jnp.where(c == 0, d, 0), 128), 128), :]
+            right, n = atr[:, pl.ds(pl.multiple_of(c * d, 128), d)], d
+        put(slice(None), 0, n, dot(left, right).reshape(8, 16, n))
+
+    def tail(u, ws):
+        if ws[1]:
+            r.stage_two(u - 1, ws[1])
+        if ws[2]:
+            r.stage_three(u - 2, ws[2])
+        if ws[3]:
+            r.stage_four(u - 3, ws[3], start_of(ws[3]))
+        if ws[4]:
+            r.stage_five(u - 4, ws[4])
+
+    def widths(u):
+        return [width(u - k) if 0 <= u - k < units else None for k in range(5)]
+
+    def step(u, kind, first, ws):
+        product(u, kind, first, False)
+        r.first(u, ws[0]).start()
+        product(u, kind, first, True)
+        tail(u, ws)
+
+    def hidden(t):
+        val = dot(dy[...], wd[pl.ds(pl.multiple_of(256 * t, 256), 256), :], 1, 1)
+        for i in (0, 1):
+            part = val[:, 128 * i:128 * i + 128]
+            for j in (0, 1):
+                at = pl.ds(pl.multiple_of(512 * t + 256 * i + 128 * j, 128), 128)
+                dgu[:, at] = (part * dgu[:, at].astype(F32)).astype(BF16)
+
+    def hidden_unit(u):
+        hidden(u)
+        tiles = mt.shape[0] // 256
+
+        @pl.when(u + 8 < tiles)
+        def _():
+            hidden(u + 8)
+
+    def input_two(j):
+        weights(j).wait()
+        val = dot(dgu[:, wide * j:wide * j + wide], wb[j % 2], 1, 1)
+        acc[...] = val if j == 0 else acc[...] + val
+        weights(j + 2).start()
+
+    def norm_two():
+        loads["h"].wait()
+        for i in range(0, rows, 128):
+            s = slice(i, i + 128)
+            v = dy[s, :].astype(F32) + norm_back_rows(h[s, :], acc[s, :])
+            dh[s, :] = v
+            atr[s, :d] = v.astype(BF16)
+
+    def mixed_grad():
+        loads["wo"].wait()
+        loads["qkv"].wait()
+        do[...] = dot(atr[:, :d], wo[...], 1, 1).astype(BF16)
+
+    def turn_back(t, s):
+        return t * cos_ref[s, :] - turn(t) * sin_ref[s, :]
+
+    def attend_back(pair):
+        lo = pl.multiple_of(pair * 128, 128)
+        lanes = [pl.ds(pl.multiple_of(lo + d * i, 128), 128) for i in range(4)]
+        for qt in reversed(range(rows // 128)):
+            n = 128 * (qt + 1)
+            s = slice(128 * qt, n)
+            keys = qkv[:n, lanes[1]]
+            q2, g2 = two_heads(qkv[s, lanes[0]]), two_heads(do[s, lanes[0]])
+            p = probabilities(q2, keys, bias_ref[:, :n])
+            dp = dot(g2, qkv[:n, lanes[2]], 1, 1)
+            ds = (p * (dp - jnp.sum(p * dp, axis=-1, keepdims=True)) * 0.125).astype(BF16)
+            new_v, new_k = dot(p.astype(BF16), g2, 0, 0), dot(ds, q2, 0, 0)
+            if n == rows:
+                dv[...] = new_v
+                dk[...] = new_k
+            else:
+                dv[:n, :] = dv[:n, :] + new_v
+                dk[:n, :] = dk[:n, :] + new_k
+            atr[s, lanes[1]] = turn_back(join_heads(dot(ds, keys)), s).astype(BF16)
+        every = slice(0, rows)
+        atr[:, lanes[2]] = turn_back(dk[...], every).astype(BF16)
+        atr[:, lanes[3]] = dv[...].astype(BF16)
+
+    def input_one(j):
+        weights(4 + j).wait()
+        val = dot(atr[:, d * (j + 1):d * (j + 2)], wb[j % 2, :, :d], 1, 1)
+        acc[...] = val if j == 0 else acc[...] + val
+        if j == 0:
+            weights(6).start()
+
+    grad_out = pltpu.make_async_copy(dh, grad_h, st_s.at[0])
+    result_out = pltpu.make_async_copy(do, out_h, st_s.at[1])
+
+    def norm_one():
+        for i in range(0, rows, 128):
+            s = slice(i, i + 128)
+            dh[s, :] = dh[s, :] + norm_back_rows(x_ref[s, :].astype(F32), acc[s, :])
+        grad_out.start()
+
+    def result(i):
+        s = slice(256 * i, 256 * i + 256)
+        do[s, :] = ((h[s, :] + dot(mt[:, s], wd[...], 0, 0)) * live[s, :]).astype(BF16)
+
+    before = {0: lambda: loads["mt"].wait(), 8: lambda: loads["bt"].wait(), 24: lambda: loads["ot"].wait(), 28: lambda: loads["at"].wait()}
+    fill = {8 + j: functools.partial(input_two, j) for j in range(4)}
+    fill[12] = norm_two
+    fill[13] = mixed_grad
+    fill.update({29 + 2 * j: functools.partial(input_one, j) for j in range(3)})
+    fill[35] = norm_one
+    fill[36] = lambda: result(0)
+    fill[37] = lambda: (result(1), result_out.start())
+    ranged = [(0, 8, hidden_unit), (14, 22, lambda u: attend_back(u - 14))]
+
+    weights(0).start()
+    weights(1).start()
+    r.barrier()
+    edges = sorted({a for a, _, _, _ in bounds} | {e for a, b, _ in ranged for e in (a, b)} | {units} | set(before))
+    u = 0
+    while u < units:
+        if u in before:
+            before[u]()
+        if u == 0:
+            ready = False
+        ws = widths(u)
+        first, _, kind, w = next(b for b in bounds if b[0] <= u < b[1])
+        in_range = next((f for a, b, f in ranged if a <= u < b), None)
+        end = min(e for e in edges if e > u)
+        plain = all(x == w for x in ws) and u not in fill
+        stop = u
+        while plain and stop < end and stop not in fill:
+            stop += 1
+        if plain and stop - u > 1:
+            def body(i, _, kind=kind, first=first, ws=ws, f=in_range):
+                step(i, kind, first, ws)
+                if f:
+                    f(i)
+                return 0
+            lax.fori_loop(u, stop, body, 0)
+            u = stop
+            continue
+        if ws[3] and u - 3 == start_of(ws[3]) and u > 3:
+            r.drain_across(u - 3, width(u - 4))
+        step(jnp.int32(u), kind, first, ws)
+        if in_range:
+            if u == 0:
+                loads["wd"].wait()
+                loads["gu"].wait()
+            in_range(jnp.int32(u))
+        if u in fill:
+            fill[u]()
+        u += 1
+    for u in range(units, units + 4):
+        tail(jnp.int32(u), widths(u))
+    r.finish(units, width)
+    grad_out.wait()
+    result_out.wait()
+
+
+def backward_call(x, dy, live, bias, cos, sin, saved, full):
+    rows, d = x.shape
+    ff = saved[3].shape[0]
+    wide = 2 * ff // 4
+    chunks = 10
+    vm, an = pl.BlockSpec(memory_space=pltpu.VMEM), pl.BlockSpec(memory_space=pl.ANY)
+    v = lambda s, t=BF16: pltpu.VMEM(s, t)
+    bufs, sems = Reduce.scratch(chunks, wide)
+    scratch = [v((2 * d, rows)), v((d, rows)), v((ff, rows)), v((rows, 3 * d)), v((rows, 2 * ff)), v((rows, d), F32), v((ff, d)), v((2, d, wide)), v((d, d)),
+               v((rows, 4 * d)), v((rows, d)), v((rows, d), F32), v((rows, d), F32), v((rows, 128), F32), v((rows, 128), F32), DMA((9,)), DMA((2,)), DMA((2,))]
+    return pl.pallas_call(
+        functools.partial(backward_kernel, wide),
+        out_shape=[jax.ShapeDtypeStruct((chunks, 4, 2, 16, wide), BF16), jax.ShapeDtypeStruct((rows, d), BF16), jax.ShapeDtypeStruct((rows, d), F32)],
+        in_specs=[vm] * 6 + [an] * 11, out_specs=[vm, an, an], scratch_shapes=scratch + bufs + sems,
+        compiler_params=pltpu.CompilerParams(collective_id=1, has_side_effects=True, vmem_limit_bytes=63 << 20),
+    )(x, dy, live, bias, cos, sin, *saved, *full)
+
+
+def pieces(total, c, w):
+    t = total[c, :, :, :, :w]
+    return jnp.stack([t[0, 0], t[2, 0], t[1, 0], t[3, 0]] + [t[i, 1] for i in range(4)])
+
+
+def unpack(total, wide, d):
+    down = [pieces(total, c, wide).reshape(8, 16, wide // 128, 128).transpose(2, 1, 0, 3).reshape(-1, d) for c in (0, 1)]
+    gate_up = [pieces(total, c, wide).reshape(128, wide) for c in (2, 3, 4, 5)]
+    attention = [pieces(total, c, d).reshape(128, d) for c in (6, 7, 8, 9)]
+    return jnp.concatenate(down, 0), jnp.concatenate(gate_up, 1), attention[0], jnp.stack(attention[1:], 1)
+
+
 def gather_full(local, rep_count, rep_index):
     rows = local.shape[0]
     flat = local.reshape(rows, -1)
@@ -118,7 +873,7 @@
     return jnp.transpose(pieces, (1, 0, 2)).reshape(rows, -1).astype(jnp.float32)
 
 
-def shards(
+def shards_generic(
     tokens,
     cotangent,
     lengths,
@@ -307,9 +1062,95 @@
     )
 
 
+def shards_fast(
+    tokens,
+    cotangent,
+    lengths,
+    slot_sequence,
+    step_count,
+    learn_rate,
+    attention_in,
+    attention_in_first,
+    attention_in_second,
+    attention_out,
+    attention_out_first,
+    attention_out_second,
+    gate_up_weight,
+    gate_up_first,
+    gate_up_second,
+    down_weight,
+    down_first,
+    down_second,
+):
+    _, rows, d = tokens.shape
+    x = tokens.reshape(rows, d)
+    matches = jnp.arange(lengths.shape[0]) == slot_sequence[0]
+    length = jnp.sum(jnp.where(matches, lengths, 0))
+    alive = jnp.arange(rows) < length
+    live = alive.astype(F32)[:, None]
+    bias = jnp.where(alive, 0.0, masked_score)[None].astype(F32)
+    dy = jnp.where(alive[:, None], cotangent.reshape(rows, d), jnp.zeros((), BF16))
+    cosine, sine = rope_tables(rows, HD)
+    sign = jnp.where(jnp.arange(HD) < HD // 2, -1.0, 1.0)
+    cosine = jnp.tile(cosine[:, 0], (1, 2))
+    sine = jnp.tile(sine[:, 0] * sign, (1, 2))
+    owned, _, ff = gate_up_weight.shape
+    tiled = gate_up_weight.reshape(owned, 2, ff // 128, 128).transpose(0, 2, 1, 3).reshape(-1, 128)
+    results = forward_call(x, bias, cosine, sine, attention_in.transpose(1, 0, 2), attention_out, tiled, down_weight)
+    full, saved = results[:4], results[4:]
+    total, output, input_grad = backward_call(x, dy, live, bias, cosine, sine, saved, full)
+    output = output.reshape(tokens.shape)
+    input_grad = input_grad.reshape(tokens.shape)
+    down_part, gate_up_part, out_part, in_part = [part.astype(F32) for part in unpack(total, ff // 2, d)]
+    gate_up_part = gate_up_part.reshape(owned, ff // 128, 2, 128).transpose(0, 2, 1, 3).reshape(owned, 2, ff)
+    in_grad, in_new, in_first, in_second = adam_update(
+        attention_in,
+        attention_in_first,
+        attention_in_second,
+        in_part,
+        step_count,
+        learn_rate,
+    )
+    out_grad, out_new, out_first, out_second = adam_update(
+        attention_out,
+        attention_out_first,
+        attention_out_second,
+        out_part,
+        step_count,
+        learn_rate,
+    )
+    gu_grad, gu_new, gu_first, gu_second = adam_update(
+        gate_up_weight, gate_up_first, gate_up_second, gate_up_part, step_count, learn_rate
+    )
+    dn_grad, dn_new, dn_first, dn_second = adam_update(
+        down_weight, down_first, down_second, down_part, step_count, learn_rate
+    )
+    return (
+        output,
+        input_grad,
+        in_grad,
+        in_new,
+        in_first,
+        in_second,
+        out_grad,
+        out_new,
+        out_first,
+        out_second,
+        gu_grad,
+        gu_new,
+        gu_first,
+        gu_second,
+        dn_grad,
+        dn_new,
+        dn_first,
+        dn_second,
+    )
+
+
 def solution(mesh):
+    fast = mesh.shape["rep"] == 4 and mesh.shape["shard"] == 8
     return jax.shard_map(
-        shards,
+        shards_fast if fast else shards_generic,
         mesh=mesh,
         in_specs=(
             P(("rep", "shard"), None, None),

time: 937 us -> 385 us (0.41)
  waiting for transfers between devices: 493 us -> 0 us
  Pallas kernels: 0 us -> 292 us
  matrix products: 169 us -> 0 us
  local copies, waits for them, and re-layouts: 134 us -> 58.9 us
  blocking collectives: 55.3 us -> 0 us
  other arithmetic: 61.3 us -> 23.4 us
  between operations: 17 us -> 3.63 us
    pallas_call x0 -> x2, Pallas kernels: none -> 292 us  [the longest x1 173 us: backward_call(): pl.pallas_call(functools.partial(backward_kernel, wide), out_shape=[jax.S...]
    all_gather x8 -> x0, waiting for transfers between devices: 248 us -> none  [the longest x4 183 us: gather_full(): return lax.all_gather(column, 'rep', axis=0, tiled=False)]
    unnamed x22 -> x0, waiting for transfers between devices: 195 us -> none
    dot_general x18 -> x0, matrix products: 169 us -> none  [the longest x1 26.2 us: attend_backward(): jnp.einsum('hqk,khd->qhd', score_grad, rotated_keys, preferred_element_ty...]
    all_gather x4 -> x0, blocking collectives: 55.3 us -> none  [the longest x3 35.9 us: reduce_full(): pieces = lax.all_gather(part, 'rep', axis=0, tiled=False)]
    reduce_scatter x2 -> x0, waiting for transfers between devices: 50.8 us -> none  [reduce_full(): part = lax.psum_scatter(part, 'shard', scatter_dimension=0, tiled=True)]
    dot_general x3 -> x0, local copies, waits for them, and re-layouts: 21.3 us -> none  [the longest x1 9.03 us: shards(): jnp.einsum('rd,qde->rqe', first_input, in_full, preferred_element_type=jn...]
    slice x6 -> x1, local copies, waits for them, and re-layouts: 21 us -> 0.67 us  [pieces(): t[i, 1]]
  transfers between devices with their start and end apart: 16 -> 0, of which waited for: 15 -> 0; matrix products, arithmetic and copies ran while one was open for 31% -> 0% of each run, Pallas kernels for 0% -> 0%
where the time goes in v3:
time: 385 us; the launch traced here: 378 us
  Pallas kernels  292 us (76%)
  local copies, waits for them, and re-layouts  58.9 us (15%)
  other arithmetic  23.4 us (6%)
    pallas_call x1, Pallas kernels, backward_call(): pl.pallas_call(functools.partial(backward_kernel, wide), out_shape=[jax.S...  173 us
    pallas_call x1, Pallas kernels, forward_call(): pl.pallas_call(functools.partial(forward_kernel, shapes, chunks), out_sha...  119 us
    unnamed x119, local copies, waits for them, and re-layouts  42.2 us
    sub x4, other arithmetic, adam_update(): weight - learn_rate[0] * (first_hat / (jnp.sqrt(second_hat) + adam_eps) +...  16.9 us

profile of v3, /device:TPU:0, one launch (start us, length us, event | category | flops | bytes accessed | tf_op | source)
XLA Modules:
  0.0 377.7 jit_solution(15632114105062396284)
XLA Ops:
  1.3 1.3 fusion.8
  2.6 1.2 compare_select_fusion.bias_ref
  5.9 4.1 %copy.54 = f32[128,2,2816]{0,2,1:T(8,128)S(1)} copy(f32[128,2,2816]{2,1,0:T(2,128)} %param.30) | data formatting | bytes 5767168 | tf_op args[12]
  10.1 3.7 copy.55
  13.8 118.8 %shard_map.313 = (bf16[1024,3072]{1,0:T(8,128)(2,1)}, bf16[1024,1024]{1,0:T(8,128)(2,1)}, bf16[1024,5632]{1,0:T(8,128)(2,1)}, bf16[2816,1024]{1,0:T(8,128)(2,1)}...) custom-call(bf16[512,1024]{1,0:T(8,128)(2,1)} %bitcast.366, ...), custom_call_target="tpu_custom_call" | custom-call | tf_op jit(solution)/shard_map/pallas_call | solution.py:460
  133.2 1.1 bitcast_select_fusion.dy
  134.3 1.4 fusion.4.live
  135.7 173.0 %shard_map.314 = (bf16[10,4,2,16,1408]{4,3,2,1,0:T(8,128)(2,1)}, bf16[512,1024]{1,0:T(8,128)(2,1)}, f32[512,1024]{1,0:T(8,128)}) custom-call(bf16[512,1024]{1,0:T(8,128)(2,1)} %bitcast.367, bf16[512,1024]{1,0:T(8,128)(2,1)} %bitcast_select_fusion.dy, f32[512,1]{1,0:T(8,128)} %fusion.4.live, f32[1,512]{1,0:T(1,128)} %compare_select_fusion.bias_ref, ...), custom_call_target="tpu_custom_call" | custom-call | tf_op jit(solution)/shard_map/pallas_call | solution.py:839
  308.8 2.7 slice_bitcast_fusion.1
  319.4 1.3 copy.70
  322.2 4.4 %multiply_subtract_fusion.2 = (f32[352,1024]{1,0:T(8,128)}, f32[352,1024]{1,0:T(8,128)}, f32[352,1024]{1,0:T(8,128)}, f32[352,1024]{1,0:T(8,128)}) fusion(f32[352,1024]{1,0:T(8,128)S(1)} %copy-done.5, f32[]{:T(128)} %bitcast.43, f32[]{:T(128)} %bitcast.42, f32[]{:T(128)} %bitcast.360, f32[352,1024]{1,0:T(8,128)S(1)} %copy-done.10, f32[352,1024]{1,0:T(8,128)} %param.34, ...), kind=kLoop, calls=%fused_computation.12 | loop fusion | flops 6848512 | bytes 10813452 | tf_op jit(solution)/shard_map/sub | solution.py:107
  328.8 1.8 copy.64
  331.6 3.3 copy.65
  335.0 5.7 %copy.66 = f32[128,2,2816]{0,2,1:T(8,128)} copy(f32[128,2,2816]{2,1,0:T(2,128)} %param.32) | data formatting | bytes 5767168 | tf_op args[14]
  340.7 6.3 %multiply_subtract_fusion = (f32[128,2,2816]{0,2,1:T(8,128)}, f32[128,2,2816]{0,2,1:T(8,128)}, f32[128,2,2816]{0,2,1:T(8,128)}) fusion(f32[128,2,2816]{0,2,1:T(8,128)S(1)} %copy-done.1, f32[]{:T(128)} %bitcast.43, f32[]{:T(128)} %bitcast.42, f32[]{:T(128)} %bitcast.359, f32[128,2,22,128]{0,3,2,1:T(8,128)} %copy.64, f32[128,2,2816]{0,2,1:T(8,128)} %copy.66, ...), kind=kLoop, calls=%fused_computation.3 | loop fusion | flops 10813440 | bytes 20185100 | tf_op jit(solution)/shard_map/sub | solution.py:107
  347.0 5.7 %copy.72 = f32[128,2,2816]{2,1,0:T(2,128)} copy(f32[128,2,2816]{0,2,1:T(8,128)} %get-tuple-element.86) | data formatting | bytes 5767168
  352.7 3.3 copy.73
  356.0 5.7 %copy.74 = f32[128,2,2816]{2,1,0:T(2,128)} copy(f32[128,2,2816]{0,2,1:T(8,128)} %get-tuple-element.87) | data formatting | bytes 5767168
  361.7 3.3 copy.71
  365.0 1.4 slice_bitcast_fusion.6
  366.8 1.1 copy-done.4
  367.9 4.7 %multiply_subtract_fusion.1 = (f32[128,3,1024]{2,0,1:T(8,128)}, f32[128,3,1024]{2,0,1:T(8,128)}, f32[128,3,1024]{2,0,1:T(8,128)}, f32[128,3,1024]{2,0,1:T(8,128)}) fusion(f32[128,3,1024]{2,0,1:T(8,128)S(1)} %copy-done.4, f32[]{:T(128)} %bitcast.43, f32[]{:T(128)} %bitcast.42, f32[]{:T(128)} %bitcast.357, f32[128,3,1024]{2,0,1:T(8,128)S(1)} %copy-done.9, ...), kind=kLoop, calls=%fused_computation.8 | loop fusion | flops 7077888 | bytes 11796492 | tf_op jit(solution)/shard_map/sub | solution.py:107
  372.6 1.5 multiply_subtract_fusion.3
  376.1 1.3 copy.157
  (149 shorter events, 15.8 us)
Async XLA Ops:
  10.0 3.7 copy-start
  13.8 119.4 %copy-start.15 = (bf16[1,512,1024]{2,1,0:T(8,128)(2,1)S(1)}, bf16[1,512,1024]{2,1,0:T(8,128)(2,1)}, u32[]{:S(2)}) copy-start(bf16[1,512,1024]{2,1,0:T(8,128)(2,1)} %param.19) | copy-start | bytes 3145732
  314.4 7.8 %copy-start.5 = (f32[352,1024]{1,0:T(8,128)S(1)}, f32[352,1024]{1,0:T(8,128)}, u32[]{:S(2)}) copy-start(f32[352,1024]{1,0:T(8,128)} %wdn_h.1) | copy-start | bytes 4325380
  314.4 7.8 %copy-start.10 = (f32[352,1024]{1,0:T(8,128)S(1)}, f32[352,1024]{1,0:T(8,128)}, u32[]{:S(2)}) copy-start(f32[352,1024]{1,0:T(8,128)} %param.35) | copy-start | bytes 4325380
  322.2 4.5 %copy-start.13 = (bf16[4,2,16,1408]{3,2,1,0:T(8,128)(2,1)S(1)}, bf16[4,2,16,1408]{3,2,1,0:T(8,128)(2,1)}, u32[]{:S(2)}) copy-start(bf16[4,2,16,1408]{3,2,1,0:T(8,128)(2,1)} %get-tuple-element.101) | copy-start | bytes 1081348
  322.2 4.6 %copy-start.14 = (bf16[4,2,16,1408]{3,2,1,0:T(8,128)(2,1)S(1)}, bf16[4,2,16,1408]{3,2,1,0:T(8,128)(2,1)}, u32[]{:S(2)}) copy-start(bf16[4,2,16,1408]{3,2,1,0:T(8,128)(2,1)} %get-tuple-element.102) | copy-start | bytes 1081348
  326.7 1.0 copy-start.11
  326.7 1.1 copy-start.12
  328.8 2.9 copy-start.6
  335.0 5.7 %copy-start.1 = (f32[128,2,2816]{0,2,1:T(8,128)S(1)}, f32[128,2,2816]{0,2,1:T(8,128)}, u32[]{:S(2)}) copy-start(f32[128,2,2816]{0,2,1:T(8,128)} %copy-done) | copy-start | bytes 8650756
  347.0 5.7 %copy-start.3 = (f32[128,2,2816]{0,2,1:T(8,128)S(1)}, f32[128,2,2816]{0,2,1:T(8,128)}, u32[]{:S(2)}) copy-start(f32[128,2,2816]{0,2,1:T(8,128)} %get-tuple-element.88) | copy-start | bytes 8650756
  356.0 5.7 %copy-start.2 = (f32[128,2,22,128]{0,3,2,1:T(8,128)S(1)}, f32[128,2,22,128]{0,3,2,1:T(8,128)}, u32[]{:S(2)}) copy-start(f32[128,2,22,128]{0,3,2,1:T(8,128)} %copy.64) | copy-start | bytes 8650756
  365.0 1.8 copy-start.9
  366.4 1.5 copy-start.4
  367.9 4.7 %copy-start.7 = (f32[128,1024]{1,0:T(8,128)S(1)}, f32[128,1024]{1,0:T(8,128)}, u32[]{:S(2)}) copy-start(f32[128,1024]{1,0:T(8,128)} %wout_h.1) | copy-start | bytes 1572868
  367.9 4.7 %copy-start.17 = (f32[128,1024]{1,0:T(8,128)S(1)}, f32[128,1024]{1,0:T(8,128)}, u32[]{:S(2)}) copy-start(f32[128,1024]{1,0:T(8,128)} %param.29) | copy-start | bytes 1572868
  367.9 4.7 %copy-start.18 = (f32[128,1024]{1,0:T(8,128)S(1)}, f32[128,1024]{1,0:T(8,128)}, u32[]{:S(2)}) copy-start(f32[128,1024]{1,0:T(8,128)} %param.28) | copy-start | bytes 1572868
  372.6 1.5 copy-start.16
  374.1 2.0 copy-start.8

commit v4 on v3

--- a/solution.py
+++ b/solution.py
@@ -2,14 +2,17 @@
 
 import jax
 import jax.numpy as jnp
+import numpy as np
 from jax import lax
 from jax.experimental import pallas as pl
+from jax.experimental.layout import Layout, with_layout_constraint
 from jax.experimental.pallas import tpu as pltpu
 from jax.sharding import PartitionSpec as P
 
 MESH = pl.DeviceIdType.MESH
 DMA = pltpu.SemaphoreType.DMA
 RING = 4
+rowwise = Layout(major_to_minor=(0, 1, 2, 3))
 F32, BF16 = jnp.float32, jnp.bfloat16
 
 HD = 64
@@ -42,6 +45,17 @@
     angles = jnp.arange(position_count, dtype=jnp.float32)[:, None] * frequency[None, :]
     angles = jnp.concatenate([angles, angles], axis=1)
     return (jnp.cos(angles)[:, None, :], jnp.sin(angles)[:, None, :])
+
+
+def half_turns(position_count, head_size):
+    half_size = head_size // 2
+    frequency = np.float32(rope_base) ** (-(np.arange(half_size, dtype=np.float32) * np.float32(2.0) / np.float32(head_size)))
+    angles = np.arange(position_count, dtype=np.float32)[:, None] * frequency[None, :]
+    cosine, sine = np.cos(angles), np.sin(angles)
+    return (
+        jnp.asarray(np.concatenate([cosine] * 4, axis=1), jnp.float32),
+        jnp.asarray(np.concatenate([-sine, sine] * 2, axis=1), jnp.float32),
+    )
 
 
 def rotate(values, cosine_table, sine_table):
@@ -267,6 +281,10 @@
     return lax.dot_general(a, b, (((da,), (db,)), ((), ())), preferred_element_type=F32)
 
 
+def key_bias(ref, length):
+    ref[...] = jnp.where(lax.broadcasted_iota(jnp.int32, ref.shape, 1) < length, 0.0, -1e30)
+
+
 def probabilities(q2, keys, bias):
     n, width = q2.shape[0] // 2, keys.shape[0]
     s = dot(q2, keys, 1, 1) * 0.125 + bias
@@ -281,10 +299,10 @@
 
 def forward_kernel(
     shapes, chunks,
-    x_ref, bias_ref, cos_ref, sin_ref, win_h, wout_h, wgu_h, wdn_h,
+    x_ref, cos_ref, sin_ref, lengths, slot, win_h, wout_h, wgu_h, wdn_h,
     fin_h, fout_h, fgu_h, fdn_h, at_h, ot_h, bt_h, mt_h, qkv_h, slopes_h, h_h,
     win, wout, wgu, wdn, lin, lout, lgu, ldn, bin_, bout, bgu,
-    a, at, qkv, o, ot, h, b, bt, mt, slopes, in_s, load_s, out_s, *sems,
+    a, at, qkv, o, ot, h, b, bt, mt, slopes, bias_ref, in_s, load_s, out_s, *sems,
 ):
     g = Gather(shapes, chunks, (lin, lout, lgu, ldn), (fin_h, fout_h, fgu_h, fdn_h), sems)
     rows = x_ref.shape[0]
@@ -295,6 +313,7 @@
         ((at, at_h), (ot, ot_h), (bt, bt_h), (mt, mt_h), (qkv, qkv_h), (slopes, slopes_h), (h, h_h)))]
     AT, OT, BT, MT, QKV, SL, H = range(7)
     g.barrier()
+    key_bias(bias_ref, lengths[slot[0]])
 
     def weight_in(t):
         loads[t].wait()
@@ -442,26 +461,26 @@
         cp.wait()
 
 
-def forward_call(x, bias, cos, sin, win, wout, wgu, wdn):
+def forward_call(x, cos, sin, lengths, slot, win, wout, wgu, wdn):
     rows, d = x.shape
     r = wout.shape[0]
     ff2 = wgu.shape[0] * 128 // r
     ff = ff2 // 2
     shapes = ((r, 3 * d), (r, d), (r, ff2), wdn.shape)
     chunks = ((0, 0, r, 0, 3 * d, 1), (1, 0, r, 0, d, 1), (2, 0, r, 0, ff, 0), (2, 0, r, ff, ff, 0), (3, 0, wdn.shape[0], 0, d, 1))
-    vm, an = pl.BlockSpec(memory_space=pltpu.VMEM), pl.BlockSpec(memory_space=pl.ANY)
+    vm, an, sm = (pl.BlockSpec(memory_space=m) for m in (pltpu.VMEM, pl.ANY, pltpu.SMEM))
     sd = lambda s, t=BF16: jax.ShapeDtypeStruct(s, t)
     v = lambda s, t=BF16: pltpu.VMEM(s, t)
     outs = [sd((8 * s[0], s[1])) for s in shapes] + [sd((d, rows)), sd((d, rows)), sd((d, rows)), sd((ff, rows)), sd((rows, 3 * d)), sd((rows, ff2)), sd((rows, d), F32)]
     scratch = [v(win.shape, F32), v(wout.shape, F32), v(wgu.shape, F32), v(wdn.shape, F32)] + [v(s) for s in shapes]
     scratch += [v((8 * r, 3 * d)), v((8 * r, d)), v((8 * r, ff2))]
-    scratch += [v((rows, d)), v((d, rows)), v((rows, 3 * d)), v((rows, d)), v((d, rows)), v((rows, d), F32), v((rows, d)), v((d, rows)), v((ff, rows)), v((rows, ff2))]
+    scratch += [v((rows, d)), v((d, rows)), v((rows, 3 * d)), v((rows, d)), v((d, rows)), v((rows, d), F32), v((rows, d)), v((d, rows)), v((ff, rows)), v((rows, ff2)), v((1, rows), F32)]
     scratch += [DMA((4,)), DMA((4,)), DMA((7,))] + Gather.scratch(4, len(chunks))
     return pl.pallas_call(
         functools.partial(forward_kernel, shapes, chunks),
-        out_shape=outs, in_specs=[vm] * 4 + [an] * 4, out_specs=[an] * len(outs), scratch_shapes=scratch,
+        out_shape=outs, in_specs=[vm] * 3 + [sm] * 2 + [an] * 4, out_specs=[an] * len(outs), scratch_shapes=scratch,
         compiler_params=pltpu.CompilerParams(collective_id=0, has_side_effects=True, vmem_limit_bytes=60 << 20),
-    )(x, bias, cos, sin, win, wout, wgu, wdn)
+    )(x, cos, sin, lengths, slot, win, wout, wgu, wdn)
 
 
 class Reduce:
@@ -610,9 +629,9 @@
 
 def backward_kernel(
     wide,
-    x_ref, dy, live, bias_ref, cos_ref, sin_ref, at_h, ot_h, bt_h, mt_h, qkv_h, slopes_h, h_h, fin_h, fout_h, fgu_h, fdn_h,
+    x_ref, cot_ref, cos_ref, sin_ref, lengths, slot, at_h, ot_h, bt_h, mt_h, qkv_h, slopes_h, h_h, fin_h, fout_h, fgu_h, fdn_h,
     total, out_h, grad_h,
-    atl, bt, mt, qkv, dgu, h, wd, wb, wo, atr, do, acc, dh, dk, dv, ld_s, wb_s, st_s, *rs,
+    atl, bt, mt, qkv, dgu, h, wd, wb, wo, atr, do, acc, dh, dk, dv, dy, bias_ref, ld_s, wb_s, st_s, *rs,
 ):
     r = Reduce(rs[:8] + (total,) + rs[8:])
     rows, d = x_ref.shape
@@ -769,7 +788,7 @@
 
     def result(i):
         s = slice(256 * i, 256 * i + 256)
-        do[s, :] = ((h[s, :] + dot(mt[:, s], wd[...], 0, 0)) * live[s, :]).astype(BF16)
+        do[s, :] = jnp.where(alive(256 * i, 256), h[s, :] + dot(mt[:, s], wd[...], 0, 0), 0.0).astype(BF16)
 
     before = {0: lambda: loads["mt"].wait(), 8: lambda: loads["bt"].wait(), 24: lambda: loads["ot"].wait(), 28: lambda: loads["at"].wait()}
     fill = {8 + j: functools.partial(input_two, j) for j in range(4)}
@@ -783,6 +802,15 @@
 
     weights(0).start()
     weights(1).start()
+    length = lengths[slot[0]]
+
+    def alive(first, n):
+        return lax.broadcasted_iota(jnp.int32, (n, d), 0) + first < length
+
+    for i in range(0, rows, 128):
+        s = slice(i, i + 128)
+        dy[s, :] = jnp.where(alive(i, 128), cot_ref[s, :].astype(F32), 0.0).astype(BF16)
+    key_bias(bias_ref, length)
     r.barrier()
     edges = sorted({a for a, _, _, _ in bounds} | {e for a, b, _ in ranged for e in (a, b)} | {units} | set(before))
     u = 0
@@ -826,34 +854,84 @@
     result_out.wait()
 
 
-def backward_call(x, dy, live, bias, cos, sin, saved, full):
+def backward_call(x, cot, cos, sin, lengths, slot, saved, full):
     rows, d = x.shape
     ff = saved[3].shape[0]
     wide = 2 * ff // 4
     chunks = 10
-    vm, an = pl.BlockSpec(memory_space=pltpu.VMEM), pl.BlockSpec(memory_space=pl.ANY)
+    vm, an, sm = (pl.BlockSpec(memory_space=m) for m in (pltpu.VMEM, pl.ANY, pltpu.SMEM))
     v = lambda s, t=BF16: pltpu.VMEM(s, t)
     bufs, sems = Reduce.scratch(chunks, wide)
     scratch = [v((2 * d, rows)), v((d, rows)), v((ff, rows)), v((rows, 3 * d)), v((rows, 2 * ff)), v((rows, d), F32), v((ff, d)), v((2, d, wide)), v((d, d)),
-               v((rows, 4 * d)), v((rows, d)), v((rows, d), F32), v((rows, d), F32), v((rows, 128), F32), v((rows, 128), F32), DMA((9,)), DMA((2,)), DMA((2,))]
+               v((rows, 4 * d)), v((rows, d)), v((rows, d), F32), v((rows, d), F32), v((rows, 128), F32), v((rows, 128), F32), v((rows, d)), v((1, rows), F32), DMA((9,)), DMA((2,)), DMA((2,))]
     return pl.pallas_call(
         functools.partial(backward_kernel, wide),
         out_shape=[jax.ShapeDtypeStruct((chunks, 4, 2, 16, wide), BF16), jax.ShapeDtypeStruct((rows, d), BF16), jax.ShapeDtypeStruct((rows, d), F32)],
-        in_specs=[vm] * 6 + [an] * 11, out_specs=[vm, an, an], scratch_shapes=scratch + bufs + sems,
+        in_specs=[vm] * 4 + [sm] * 2 + [an] * 11, out_specs=[vm, an, an], scratch_shapes=scratch + bufs + sems,
         compiler_params=pltpu.CompilerParams(collective_id=1, has_side_effects=True, vmem_limit_bytes=63 << 20),
-    )(x, dy, live, bias, cos, sin, *saved, *full)
-
-
-def pieces(total, c, w):
-    t = total[c, :, :, :, :w]
-    return jnp.stack([t[0, 0], t[2, 0], t[1, 0], t[3, 0]] + [t[i, 1] for i in range(4)])
-
-
-def unpack(total, wide, d):
-    down = [pieces(total, c, wide).reshape(8, 16, wide // 128, 128).transpose(2, 1, 0, 3).reshape(-1, d) for c in (0, 1)]
-    gate_up = [pieces(total, c, wide).reshape(128, wide) for c in (2, 3, 4, 5)]
-    attention = [pieces(total, c, d).reshape(128, d) for c in (6, 7, 8, 9)]
-    return jnp.concatenate(down, 0), jnp.concatenate(gate_up, 1), attention[0], jnp.stack(attention[1:], 1)
+    )(x, cot, cos, sin, lengths, slot, *saved, *full)
+
+
+def adam_kernel(scalars, total, *refs):
+    masters, outs, spread = refs[:12], refs[12:28], refs[28]
+    first_scale, second_scale, rate = scalars[0], scalars[1], scalars[2]
+    wide = total.shape[-1]
+    cols = wide // 128
+    d = masters[3].shape[1]
+
+    def update(k, at, grad):
+        w, m, v = (masters[3 * k + j][at] for j in range(3))
+        m = beta_first * m + (1.0 - beta_first) * grad
+        v = beta_second * v + (1.0 - beta_second) * grad * grad
+        outs[4 * k][at] = grad
+        outs[4 * k + 1][at] = w - rate * (m * first_scale / (jnp.sqrt(v * second_scale) + adam_eps) + weight_decay * w)
+        outs[4 * k + 2][at] = m
+        outs[4 * k + 3][at] = v
+
+    def piece(c, lo, n):
+        return total[c, 0, 0, :, lo:lo + n].astype(F32)
+
+    for p in range(3):
+        update(0, (p,), piece(7 + p, 0, d))
+    update(1, (slice(None),), piece(6, 0, d))
+    stride = 4 * cols
+    for c in range(4):
+        for j in range(cols):
+            spread[pl.ds(c * cols + j, 16, stride=stride), :] = piece(2 + c, 128 * j, 128)
+    for i in range(0, 16 * stride, 176):
+        s = (slice(i, i + 176),)
+        update(2, s, spread[s])
+    half = 16 * cols
+    for c in (0, 1):
+        for j in range(cols):
+            update(3, (slice(c * half + 16 * j, c * half + 16 * j + 16),), piece(c, 128 * j, 128))
+
+
+def adam_call(scalars, total, masters):
+    chunks, _, _, _, wide = total.shape
+    blocks = []
+    for k, shape in enumerate((masters[0].shape, masters[3].shape, masters[6].shape, masters[9].shape)):
+        if k == 0:
+            blocks.append(pl.BlockSpec((3, shape[1] // 8, shape[2]), lambda i: (0, i, 0)))
+        elif k < 3:
+            blocks.append(pl.BlockSpec((shape[0] // 8, shape[1]), lambda i: (i, 0)))
+        else:
+            blocks.append(pl.BlockSpec((shape[0], shape[1] // 8), lambda i: (0, i)))
+
+    def part(i):
+        low = lax.rem(i, 2) * 2 + i // 2
+        return (0, jnp.where(i < 4, low, i - 4), i // 4, 0, 0)
+
+    shapes = [masters[3 * k].shape for k in range(4) for _ in range(4)]
+    return pl.pallas_call(
+        adam_kernel,
+        grid=(8,),
+        out_shape=[jax.ShapeDtypeStruct(s, F32) for s in shapes],
+        in_specs=[pl.BlockSpec(memory_space=pltpu.SMEM), pl.BlockSpec((chunks, 1, 1, 16, wide), part)] + [blocks[k] for k in range(4) for _ in range(3)],
+        out_specs=[blocks[k] for k in range(4) for _ in range(4)],
+        scratch_shapes=[pltpu.VMEM((masters[6].shape[0] // 8, 128), F32)],
+        compiler_params=pltpu.CompilerParams(vmem_limit_bytes=60 << 20),
+    )(scalars, total, *masters)
 
 
 def gather_full(local, rep_count, rep_index):
@@ -1084,66 +1162,34 @@
 ):
     _, rows, d = tokens.shape
     x = tokens.reshape(rows, d)
-    matches = jnp.arange(lengths.shape[0]) == slot_sequence[0]
-    length = jnp.sum(jnp.where(matches, lengths, 0))
-    alive = jnp.arange(rows) < length
-    live = alive.astype(F32)[:, None]
-    bias = jnp.where(alive, 0.0, masked_score)[None].astype(F32)
-    dy = jnp.where(alive[:, None], cotangent.reshape(rows, d), jnp.zeros((), BF16))
-    cosine, sine = rope_tables(rows, HD)
-    sign = jnp.where(jnp.arange(HD) < HD // 2, -1.0, 1.0)
-    cosine = jnp.tile(cosine[:, 0], (1, 2))
-    sine = jnp.tile(sine[:, 0] * sign, (1, 2))
+    cosine, sine = half_turns(rows, HD)
     owned, _, ff = gate_up_weight.shape
-    tiled = gate_up_weight.reshape(owned, 2, ff // 128, 128).transpose(0, 2, 1, 3).reshape(-1, 128)
-    results = forward_call(x, bias, cosine, sine, attention_in.transpose(1, 0, 2), attention_out, tiled, down_weight)
+    tiles = ff // 128
+
+    def tiled(value):
+        value = value.reshape(owned, 2, tiles, 128).transpose(0, 2, 1, 3)
+        return with_layout_constraint(value, rowwise).reshape(-1, 128)
+
+    def untiled(value):
+        value = with_layout_constraint(value.reshape(owned, tiles, 2, 128), rowwise)
+        return value.transpose(0, 2, 1, 3).reshape(owned, 2, ff)
+
+    heads = [value.transpose(1, 0, 2) for value in (attention_in, attention_in_first, attention_in_second)]
+    gates = [tiled(value) for value in (gate_up_weight, gate_up_first, gate_up_second)]
+    results = forward_call(x, cosine, sine, lengths, slot_sequence, heads[0], attention_out, gates[0], down_weight)
     full, saved = results[:4], results[4:]
-    total, output, input_grad = backward_call(x, dy, live, bias, cosine, sine, saved, full)
-    output = output.reshape(tokens.shape)
-    input_grad = input_grad.reshape(tokens.shape)
-    down_part, gate_up_part, out_part, in_part = [part.astype(F32) for part in unpack(total, ff // 2, d)]
-    gate_up_part = gate_up_part.reshape(owned, ff // 128, 2, 128).transpose(0, 2, 1, 3).reshape(owned, 2, ff)
-    in_grad, in_new, in_first, in_second = adam_update(
-        attention_in,
-        attention_in_first,
-        attention_in_second,
-        in_part,
-        step_count,
-        learn_rate,
-    )
-    out_grad, out_new, out_first, out_second = adam_update(
-        attention_out,
-        attention_out_first,
-        attention_out_second,
-        out_part,
-        step_count,
-        learn_rate,
-    )
-    gu_grad, gu_new, gu_first, gu_second = adam_update(
-        gate_up_weight, gate_up_first, gate_up_second, gate_up_part, step_count, learn_rate
-    )
-    dn_grad, dn_new, dn_first, dn_second = adam_update(
-        down_weight, down_first, down_second, down_part, step_count, learn_rate
-    )
+    total, output, input_grad = backward_call(x, cotangent.reshape(rows, d), cosine, sine, lengths, slot_sequence, saved, full)
+    steps_taken = step_count[0].astype(F32)
+    scalars = jnp.stack([1.0 / (1.0 - beta_first**steps_taken), 1.0 / (1.0 - beta_second**steps_taken), learn_rate[0]])
+    masters = heads + [attention_out, attention_out_first, attention_out_second] + gates + [down_weight, down_first, down_second]
+    new = adam_call(scalars, total, masters)
     return (
-        output,
-        input_grad,
-        in_grad,
-        in_new,
-        in_first,
-        in_second,
-        out_grad,
-        out_new,
-        out_first,
-        out_second,
-        gu_grad,
-        gu_new,
-        gu_first,
-        gu_second,
-        dn_grad,
-        dn_new,
-        dn_first,
-        dn_second,
+        output.reshape(tokens.shape),
+        input_grad.reshape(tokens.shape),
+        *[value.transpose(1, 0, 2) for value in new[:4]],
+        *new[4:8],
+        *[untiled(value) for value in new[8:12]],
+        *new[12:],
     )
 
 

time: 385 us -> 324 us (0.84)
  local copies, waits for them, and re-layouts: 58.9 us -> 3.27 us
  other arithmetic: 23.4 us -> 0.59 us
  Pallas kernels: 292 us -> 311 us
    unnamed x119 -> x6, local copies, waits for them, and re-layouts: 42.2 us -> 3.27 us
    pallas_call x0 -> x1, Pallas kernels: none -> 19.5 us  [adam_call(): pl.pallas_call(adam_kernel, grid=(8,), out_shape=[jax.ShapeDtypeStruct(s,...]
    sub x4 -> x0, other arithmetic: 16.9 us -> none  [adam_update(): weight - learn_rate[0] * (first_hat / (jnp.sqrt(second_hat) + adam_eps) +...]
    transpose x3 -> x0, local copies, waits for them, and re-layouts: 5.27 us -> none  [the longest x1 3.72 us: shards_fast(): gate_up_weight.reshape(owned, 2, ff // 128, 128).transpose(0, 2, 1, 3)]
    squeeze x2 -> x0, local copies, waits for them, and re-layouts: 4.05 us -> none  [pieces(): t = total[c, :, :, :, :w]]
    another operation x26 -> x0, local copies, waits for them, and re-layouts: 4.05 us -> none  [the longest x22 2.34 us: pieces(): jnp.stack([t[0, 0], t[2, 0], t[1, 0], t[3, 0]] + [t[i, 1] for i in range(...]
where the time goes in v4:
time: 324 us; the launch traced here: 318 us
  Pallas kernels  311 us (96%)
  local copies, waits for them, and re-layouts  3.27 us (1%)
    pallas_call x1, Pallas kernels, backward_call(): pl.pallas_call(functools.partial(backward_kernel, wide), out_shape=[jax.S...  173 us
    pallas_call x1, Pallas kernels, forward_call(): pl.pallas_call(functools.partial(forward_kernel, shapes, chunks), out_sha...  119 us
    pallas_call x1, Pallas kernels, adam_call(): pl.pallas_call(adam_kernel, grid=(8,), out_shape=[jax.ShapeDtypeStruct(s,...  19.5 us

profile of v4, /device:TPU:0, one launch (start us, length us, event | category | flops | bytes accessed | tf_op | source)
XLA Modules:
  0.0 318.2 jit_solution(1511747857198544)
XLA Ops:
  1.3 118.9 %shard_map.331 = (bf16[1024,3072]{1,0:T(8,128)(2,1)}, bf16[1024,1024]{1,0:T(8,128)(2,1)}, bf16[1024,5632]{1,0:T(8,128)(2,1)}, bf16[2816,1024]{1,0:T(8,128)(2,1)}...) custom-call(bf16[512,1024]{1,0:T(8,128)(2,1)} %bitcast.50, ...), custom_call_target="tpu_custom_call" | custom-call | tf_op jit(solution)/shard_map/pallas_call | solution.py:479
  120.2 173.0 %shard_map.332 = (bf16[10,4,2,16,1408]{4,3,2,1,0:T(8,128)(2,1)}, bf16[512,1024]{1,0:T(8,128)(2,1)}, f32[512,1024]{1,0:T(8,128)}) custom-call(bf16[512,1024]{1,0:T(8,128)(2,1)} %bitcast.51, bf16[512,1024]{1,0:T(8,128)(2,1)} %bitcast.57, f32[512,128]{1,0:T(8,128)} %constant.16.clone.cos_ref, f32[512,128]{1,0:T(8,128)} %constant.17.clone.sin_ref, s32[32]{0:T(128)} %lengths.3, ...), custom_call_target="tpu_custom_call" | custom-call | tf_op jit(solution)/shard_map/pallas_call | solution.py:867
  294.6 0.6 pad_maximum_fusion.scalars
  295.2 0.0 copy-start.1
  295.2 19.5 %shard_map.333 = (f32[3,128,1024]{2,1,0:T(8,128)}, f32[3,128,1024]{2,1,0:T(8,128)}, f32[3,128,1024]{2,1,0:T(8,128)}, f32[3,128,1024]{2,1,0:T(8,128)}, f32[128,10...) custom-call(f32[3]{0:T(128)} %pad_maximum_fusion.scalars, ...), custom_call_target="tpu_custom_call" | custom-call | tf_op jit(solution)/shard_map/pallas_call | solution.py:926
  314.7 0.0 copy-start
  314.7 0.0 copy-done.1
  314.7 1.0 copy.43
  315.7 1.0 copy-done
  316.7 1.3 copy.44
Async XLA Ops:
  295.2 19.5 %copy-start.1 = (bf16[512,1024]{1,0:T(8,128)(2,1)S(1)}, bf16[512,1024]{1,0:T(8,128)(2,1)}, u32[]{:S(2)}) copy-start(bf16[512,1024]{1,0:T(8,128)(2,1)} %get-tuple-element.59) | copy-start | bytes 3145732
  314.7 2.0 copy-start
